TPU v7x, 128 devices: a whole 4x4x4 slice. The times are simulated.
128 devices in a mesh: rep: 8 (over z, core), tab: 16 (over x, y).
Axes of the slice: x: 4, y: 4, z: 4, core: 2. Of those that a mesh axis runs over, the one named last changes fastest.
Arguments:
- inputs: bfloat16 [16384, 4096], P(('rep', 'tab')), may hold values from -24 to 24
- grad_out: bfloat16 [16384, 4096], P(('rep', 'tab')), may hold values from -6 to 6
- query_weight: bfloat16 [4096, 1024], replicated, may hold values from -0.09375 to 0.09375
- sub_keys: bfloat16 [1024, 1024], replicated, may hold values from -6 to 6
- values: bfloat16 [4096, 4096], P('tab'), may hold values from -0.09375 to 0.09375
- owner: int32 [16384, 2, 1], P(('rep', 'tab')), may hold values from 0 to 15; in each aligned block of 256 rows (0 to 255, 256 to 511, ..., all dimensions but the last counted through in order) at most 32 rows name the same one
- slot_rows: int32 [16384, 2, 32], P(('rep', 'tab')), may hold values from 0 to 255, as said below
- sub_index: int32 [16384, 2, 2, 32], P(('rep', 'tab')), may hold values from 0 to 1023
Outputs:
- input_grad: bfloat16 [16384, 4096], P(('rep', 'tab'))
- weight_grad: float32 [4096, 1024], P('tab')
- key_grad: float32 [1024, 1024], P('tab')
- table_grad: bfloat16 [4096, 4096], P('tab')
Inputs may be any that keep to these rules, and one draw needn't show every extreme that they name: `owner`: within the token-head pairs of one device (aligned blocks of 256 pairs), no shard number appears more than 32 times, and one appears exactly 32 times in some or all blocks. `slot_rows`: the 32 row numbers of one token and head are distinct.
All inputs are finite; a program needn't handle non-finite values.
Results may differ from a plain program's by a relative error of at most 0.0059.
Values may be sent and summed in bfloat16 or wider, within the bound.
A program may use at most 192 MiB of HBM per device.

v0:
```python
import math

import jax
import jax.numpy as jnp
from jax import lax
from jax.sharding import PartitionSpec as P


def weight_term(input_blocks, query_grad):
    return jnp.einsum("tgd,tk->gdk", input_blocks, query_grad, preferred_element_type=jnp.float32)


def key_term(grad_blocks, query_blocks, many, width):
    key_part = jnp.einsum(
        "tbgs,tbc->gsbc", grad_blocks, query_blocks, preferred_element_type=jnp.float32
    )
    return key_part.reshape(many, key_part.shape[1], width)


def grad_term(input_blocks, grad_blocks, query_grad, query_blocks, many):
    weight_part = weight_term(input_blocks, query_grad)
    key_part = key_term(grad_blocks, query_blocks, many, weight_part.shape[2])
    joined = jnp.concatenate([weight_part, key_part], axis=1)
    return joined.reshape(many * joined.shape[1], weight_part.shape[2])


def on_device(inputs, grad_out, query_weight, sub_keys, values, owner, slot_rows, sub_index):
    tokens = inputs.shape[0]
    model_width = inputs.shape[1]
    query_cols = query_weight.shape[1]
    key_count = sub_keys.shape[0]
    head_count = slot_rows.shape[1]
    top_count = slot_rows.shape[2]
    blocks = 2 * head_count
    half_width = query_cols // blocks
    shards = lax.axis_size("tab")
    table_rows = values.shape[0]
    capacity = 2 * tokens * head_count // shards
    messages = tokens * head_count
    slots = shards * capacity
    block_tokens = math.gcd(tokens, 64)
    block_count = tokens // block_tokens
    key_iota = jnp.arange(key_count, dtype=jnp.int32)
    query = jnp.dot(inputs, query_weight, preferred_element_type=jnp.float32)
    low_query = query.astype(jnp.bfloat16)
    query_blocks = low_query.reshape(tokens, blocks, half_width)
    key_blocks = sub_keys.reshape(key_count, blocks, half_width)
    key_wide = sub_keys.astype(jnp.float32).reshape(key_count, blocks, half_width)
    half_scores = jnp.einsum(
        "tbc,nbc->tbn",
        query.reshape(tokens, blocks, half_width),
        key_wide,
        precision=lax.Precision.HIGHEST,
    )
    picks = sub_index.reshape(tokens, blocks, top_count)

    def pick_block(pair):
        block_scores, block_picks = pair
        equal = block_picks[:, :, :, None] == key_iota[None, None, None, :]
        return jnp.sum(jnp.where(equal, block_scores[:, :, None, :], 0.0), axis=3)

    chosen = lax.map(
        pick_block,
        (
            half_scores.reshape(block_count, block_tokens, blocks, key_count),
            picks.reshape(block_count, block_tokens, blocks, top_count),
        ),
    )
    chosen = chosen.reshape(tokens, head_count, 2, top_count)
    scores = chosen[:, :, 0] + chosen[:, :, 1]
    weights = jax.nn.softmax(scores, axis=-1)
    low_weights = weights.astype(jnp.bfloat16)
    target = owner.reshape(messages)
    onehot = (target[:, None] == jnp.arange(shards, dtype=jnp.int32)[None, :]).astype(jnp.float32)
    message_iota = jnp.arange(messages, dtype=jnp.int32)
    lower = (message_iota[:, None] > message_iota[None, :]).astype(jnp.float32)
    before = jnp.dot(lower, onehot, precision=lax.Precision.HIGHEST)
    position = jnp.sum(before * onehot, axis=1).astype(jnp.int32)
    slot_of = target * capacity + position
    dispatch = jnp.arange(slots, dtype=jnp.int32)[:, None] == slot_of[None, :]
    token_dispatch = jnp.any(dispatch.reshape(slots, tokens, head_count), axis=2).astype(
        jnp.bfloat16
    )
    payload = jnp.dot(token_dispatch, grad_out, preferred_element_type=jnp.float32).astype(
        jnp.bfloat16
    )
    dispatch_wide = dispatch.astype(jnp.float32)
    send_rows = jnp.dot(
        dispatch_wide,
        slot_rows.reshape(messages, top_count).astype(jnp.float32),
        precision=lax.Precision.HIGHEST,
    ).astype(jnp.int32)
    send_weights = jnp.dot(
        dispatch.astype(jnp.bfloat16),
        low_weights.reshape(messages, top_count),
        preferred_element_type=jnp.float32,
    ).astype(jnp.bfloat16)
    arrived, arrived_index, arrived_weights = (
        lax.all_to_all(
            payload.reshape(shards, capacity, model_width),
            "tab",
            split_axis=0,
            concat_axis=0,
            tiled=True,
        ),
        lax.all_to_all(
            send_rows.reshape(shards, capacity, top_count),
            "tab",
            split_axis=0,
            concat_axis=0,
            tiled=True,
        ),
        lax.all_to_all(
            send_weights.reshape(shards, capacity, top_count),
            "tab",
            split_axis=0,
            concat_axis=0,
            tiled=True,
        ),
    )
    arrived = arrived.reshape(slots, model_width)
    arrived_index = arrived_index.reshape(slots, top_count)
    arrived_weights = arrived_weights.reshape(slots, top_count)
    products = lax.dot_general(
        arrived, values, (((1,), (1,)), ((), ())), preferred_element_type=jnp.float32
    )
    table_iota = jnp.arange(table_rows, dtype=jnp.int32)
    matches = arrived_index[:, :, None] == table_iota[None, None, :]
    slot_back = jnp.sum(jnp.where(matches, products[:, None, :], 0.0), axis=2)
    spread_table = jnp.sum(
        jnp.where(matches, arrived_weights[:, :, None].astype(jnp.float32), 0.0), axis=1
    ).astype(jnp.bfloat16)
    table_part = lax.dot_general(
        spread_table, arrived, (((0,), (0,)), ((), ())), preferred_element_type=jnp.float32
    )
    returned = lax.all_to_all(
        slot_back.reshape(shards, capacity, top_count),
        "tab",
        split_axis=0,
        concat_axis=0,
        tiled=True,
    )
    slot_grad = lax.dot_general(
        dispatch_wide,
        returned.reshape(slots, top_count),
        (((0,), (0,)), ((), ())),
        precision=lax.Precision.HIGHEST,
    ).reshape(tokens, head_count, top_count)
    score_grad = weights * (slot_grad - jnp.sum(weights * slot_grad, axis=-1, keepdims=True))
    spread_grad = jnp.broadcast_to(
        score_grad[:, :, None, :], (tokens, head_count, 2, top_count)
    ).reshape(tokens, blocks, top_count)

    def place_block(pair):
        block_spread, block_picks = pair
        equal = block_picks[:, :, :, None] == key_iota[None, None, None, :]
        return jnp.sum(jnp.where(equal, block_spread[:, :, :, None], 0.0), axis=2)

    half_grad = lax.map(
        place_block,
        (
            spread_grad.reshape(block_count, block_tokens, blocks, top_count),
            picks.reshape(block_count, block_tokens, blocks, top_count),
        ),
    )
    half_grad = half_grad.reshape(tokens, blocks, key_count).astype(jnp.bfloat16)
    query_grad = (
        jnp.einsum("tbn,nbc->tbc", half_grad, key_blocks, preferred_element_type=jnp.float32)
        .astype(jnp.bfloat16)
        .reshape(tokens, query_cols)
    )
    input_grad = lax.dot_general(
        query_grad, query_weight, (((1,), (1,)), ((), ())), preferred_element_type=jnp.float32
    ).astype(jnp.bfloat16)
    weight_rows = model_width // shards
    key_rows = key_count // shards
    per_device = weight_rows + key_rows
    input_blocks = inputs.reshape(tokens, shards, weight_rows)
    grad_blocks = half_grad.reshape(tokens, blocks, shards, key_rows)
    local = lax.psum_scatter(
        grad_term(
            input_blocks,
            grad_blocks,
            query_grad,
            query_blocks,
            per_device * lax.axis_size("tab") // per_device,
        ),
        "tab",
        scatter_dimension=0,
        tiled=True,
    )
    local_sum, table_sum = lax.psum((local, table_part), "rep")
    weight_grad = local_sum[:weight_rows]
    key_grad = local_sum[weight_rows:]
    return (input_grad, weight_grad, key_grad, table_sum.astype(jnp.bfloat16))


def solution(mesh):
    placed = (
        P(("rep", "tab"), None),
        P(("rep", "tab"), None),
        P(),
        P(),
        P("tab", None),
        P(("rep", "tab"), None, None),
        P(("rep", "tab"), None, None),
        P(("rep", "tab"), None, None, None),
    )
    return jax.shard_map(
        on_device,
        mesh=mesh,
        in_specs=placed,
        out_specs=(P(("rep", "tab"), None), P("tab", None), P("tab", None), P("tab", None)),
        check_vma=False,
    )
```

profile of v0, /device:TPU:1, one launch (start us, length us, event | category | flops | bytes accessed | tf_op | source)
XLA Modules:
  0.0 425.1 jit_solution(7707619019839026984)
XLA Ops:
  8.4 5.8 %fusion.36 = (bf16[128,1024]{1,0:T(8,128)(2,1)}, f32[128,1024]{1,0:T(8,128)S(1)}) fusion(bf16[128,4096]{1,0:T(8,128)(2,1)} %param.12, bf16[4096,1024]{1,0:T(8,128)(2,1)} %param.14), kind=kOutput, calls=%fused_computation.62 | convolution fusion | flops 1073872896 | bytes 10223616 | tf_op jit(solution)/shard_map/dot_general | solution.py:44
  14.2 3.5 fusion.6
  17.7 16.5 %while.22 = (s32[]{:T(128)}, f32[2,64,4,32]{3,2,1,0:T(4,128)}, s32[2,64,4,32]{3,2,1,0:T(4,128)S(1)}, f32[2,64,4,1024]{3,1,0,2:T(8,128)}, s32[]{:T(128)}) while((s32[]{:T(128)}, f32[2,64,4,32]{3,2,1,0:T(4,128)}, s32[2,64,4,32]{3,2,1,0:T(4,128)S(1)}, f32[2,64,4,1024]{3,1,0,2:T(8,128)}, s32[]{:T(128)}) %tuple.62), condition=%wide.region_2.3_spmd.clone, body=%wide.region_0.2_spmd.clone.sunk | while | flops 25157632 | bytes 5538373 | solution.py:62
  19.7 5.5 %select_reduce_fusion.6 = f32[64,4,32]{2,1,0:T(4,128)S(1)} fusion(f32[64,4,1024]{2,1,0:T(4,128)S(1)} %bitcast.121, s32[64,4,32]{2,1,0:T(4,128)S(1)} %dynamic-slice_bitcast_fusion.6), kind=kLoop, calls=%fused_computation.3.clone.1 | loop fusion | flops 25157632 | bytes 1114112 | tf_op jit(solution)/shard_map/while/body/eval_jaxpr/reduce_sum | solution.py:60
  27.9 5.5 %select_reduce_fusion.6 = f32[64,4,32]{2,1,0:T(4,128)S(1)} fusion(f32[64,4,1024]{2,1,0:T(4,128)S(1)} %bitcast.121, s32[64,4,32]{2,1,0:T(4,128)S(1)} %dynamic-slice_bitcast_fusion.6), kind=kLoop, calls=%fused_computation.3.clone.1 | loop fusion | flops 25157632 | bytes 1114112 | tf_op jit(solution)/shard_map/while/body/eval_jaxpr/reduce_sum | solution.py:60
  34.2 2.0 fusion.35
  48.8 7.6 %all-to-all-start.3 = ((bf16[16,2,512]{2,1,0:T(2,128)(2,1)}), bf16[16,2,512]{2,1,0:T(2,128)(2,1)S(1)}, u32[]{:S(2)}, u32[]{:S(2)}) async-start(bf16[16,2,512]{2,1,0:T(2,128)(2,1)} %reshape.169), calls=%async_computation.4 | async-start | bytes 65536 | tf_op jit(solution)/shard_map/all_to_all | solution.py:113
  60.0 1.9 convolution_convert_fusion.2
  66.8 1.7 copy.196
  68.5 1.7 reshape.171
  70.3 6.7 %all-to-all-start = ((s32[16,1,1024]{2,1,0:T(1,128)}), s32[16,1,1024]{2,1,0:T(1,128)}, u32[]{:S(2)}, u32[]{:S(2)}) async-start(s32[16,1,1024]{2,1,0:T(1,128)} %reshape.171), calls=%async_computation | async-start | bytes 131072 | tf_op jit(solution)/shard_map/all_to_all | solution.py:106
  77.0 3.2 convolution_convert_fusion
  80.2 3.4 all-to-all-done
  83.6 4.5 %all-to-all-start.1 = ((bf16[16,32,4096]{2,1,0:T(8,128)(2,1)}), bf16[16,32,4096]{2,1,0:T(8,128)(2,1)}, u32[]{:S(2)}, u32[]{:S(2)}) async-start(bf16[16,32,4096]{2,1,0:T(8,128)(2,1)} %bitcast.123), calls=%async_computation.1 | async-start | bytes 8388608 | tf_op jit(solution)/shard_map/all_to_all | solution.py:99
  92.2 46.5 %all-to-all-done.1 = bf16[16,32,4096]{2,1,0:T(8,128)(2,1)} async-done(((bf16[16,32,4096]{2,1,0:T(8,128)(2,1)}), bf16[16,32,4096]{2,1,0:T(8,128)(2,1)}, u32[]{:S(2)}, u32[]{:S(2)}) %all-to-all-start.1) | async-done | bytes 4194336 | tf_op jit(solution)/shard_map/all_to_all | solution.py:99
  138.7 3.6 fusion.37
  142.3 10.9 %select_reduce_fusion.2 = (bf16[512,256]{1,0:T(8,128)(2,1)}, f32[512,32]{1,0:T(8,128)S(1)}) fusion(f32[512,32]{1,0:T(8,128)} %bitcast.142, s32[512,32]{1,0:T(8,128)S(1)} %bitcast.143, f32[512,256]{1,0:T(8,128)S(1)} %fusion.37), kind=kLoop, calls=%fused_computation.14 | loop fusion | flops 20824064 | bytes 983040 | tf_op jit(solution)/shard_map/reduce_sum | solution.py:130
  154.1 5.3 %all-to-all-start.2 = ((f32[16,1,1024]{2,1,0:T(1,128)}), f32[16,1,1024]{2,1,0:T(1,128)S(1)}, u32[]{:S(2)}, u32[]{:S(2)}) async-start(f32[16,1,1024]{2,1,0:T(1,128)} %reshape.173), calls=%async_computation.2 | async-start | bytes 131072 | tf_op jit(solution)/shard_map/all_to_all | solution.py:136
  161.3 4.7 %all-to-all-done.2 = f32[16,1,1024]{2,1,0:T(1,128)S(1)} async-done(((f32[16,1,1024]{2,1,0:T(1,128)}), f32[16,1,1024]{2,1,0:T(1,128)S(1)}, u32[]{:S(2)}, u32[]{:S(2)}) %all-to-all-start.2) | async-done | bytes 65568 | tf_op jit(solution)/shard_map/all_to_all | solution.py:136
  168.3 17.1 %while.23 = (s32[]{:T(128)}, bf16[2,64,4,1024]{3,2,1,0:T(4,128)(2,1)S(1)}, s32[2,64,4,32]{3,2,1,0:T(4,128)S(1)}, f32[2,64,4,32]{3,2,1,0:T(4,128)S(1)}, s32[]{:T(128)}) while((s32[]{:T(128)}, bf16[2,64,4,1024]{3,2,1,0:T(4,128)(2,1)S(1)}, s32[2,64,4,32]{3,2,1,0:T(4,128)S(1)}, f32[2,64,4,32]{3,2,1,0:T(4,128)S(1)}, s32[]{:T(128)}) %tuple.64), condition=%wide.region_11.12_spmd.clone, body=%wide.region_9.11_spmd.clone.sunk | while | flops 24903680 | bytes 1769545 | solution.py:159
  168.4 8.3 %select_reduce_fusion.7 = bf16[64,4,1024]{2,1,0:T(4,128)(2,1)S(1)} fusion(f32[64,4,32]{2,1,0:T(4,128)S(1)} %dynamic-slice_bitcast_fusion.7, s32[64,4,32]{2,1,0:T(4,128)S(1)} %dynamic-slice_bitcast_fusion.8), kind=kLoop, calls=%fused_computation.9.clone.1 | loop fusion | flops 24903680 | bytes 589824 | tf_op jit(solution)/shard_map/while/body/eval_jaxpr/reduce_sum | solution.py:157
  176.9 8.3 %select_reduce_fusion.7 = bf16[64,4,1024]{2,1,0:T(4,128)(2,1)S(1)} fusion(f32[64,4,32]{2,1,0:T(4,128)S(1)} %dynamic-slice_bitcast_fusion.7, s32[64,4,32]{2,1,0:T(4,128)S(1)} %dynamic-slice_bitcast_fusion.8), kind=kLoop, calls=%fused_computation.9.clone.1 | loop fusion | flops 24903680 | bytes 589824 | tf_op jit(solution)/shard_map/while/body/eval_jaxpr/reduce_sum | solution.py:157
  186.4 3.1 reshape.168
  189.5 2.5 fusion.13
  192.2 2.2 copy.137
  197.3 2.3 convolution_bitcast_fusion
  199.6 9.2 %pad_maximum_fusion = f32[16,320,1024]{2,1,0:T(8,128)} fusion(f32[16,64,1024]{2,1,0:T(8,128)S(1)} %bitcast.125, f32[16,256,1024]{2,1,0:T(8,128)S(1)} %convolution_bitcast_fusion), kind=kLoop, calls=%fused_computation.13 | loop fusion | flops 5242880 | bytes 41943040 | tf_op jit(solution)/shard_map/concatenate | solution.py:23
  209.8 5.4 %fusion.38 = f32[256,4096]{1,0:T(8,128)} fusion(bf16[512,256]{1,0:T(8,128)(2,1)S(1)} %copy-done.5, bf16[512,4096]{1,0:T(8,128)(2,1)} %bitcast.9), kind=kOutput, calls=%fused_computation.66 | convolution fusion | flops 1073741824 | bytes 8650752 | tf_op jit(solution)/shard_map/dot_general | solution.py:133
  215.2 129.2 %reduce-scatter.2.cloned.1.call-done = f32[320,1024]{1,0:T(8,128)} async-done(((f32[5120,1024]{1,0:T(8,128)}), f32[320,1024]{1,0:T(8,128)}) %reduce-scatter.2.cloned.1.call-update) | async-done | bytes 1310736 | tf_op jit(solution)/shard_map/reduce_scatter | solution.py:180
  344.4 62.4 %all-reduce.4 = bf16[256,4096]{1,0:T(8,128)(2,1)} all-reduce(f32[256,4096]{1,0:T(8,128)} %fusion.38), channel_id=1, replica_groups=mesh['rep'=8,'tab'=16] {'rep'}, use_global_device_ids=true, to_apply=%region_15.16 | all-reduce | flops 1048576 | bytes 6291456 | tf_op jit(solution)/shard_map/psum | solution.py:192
  406.8 7.4 %convolution_convert_fusion.1 = bf16[128,4096]{1,0:T(8,128)(2,1)} fusion(bf16[128,1024]{0,1:T(8,128)(2,1)S(1)} %bitcast.132, bf16[4096,1024]{1,0:T(8,128)(2,1)} %param.14), kind=kOutput, calls=%fused_computation.19 | convolution fusion | flops 1074266112 | bytes 9699328 | tf_op jit(solution)/shard_map/dot_general | solution.py:172
  414.3 2.3 slice.18
  (94 shorter events, 43.9 us)
Async XLA Ops:
  7.2 131.5 %copy-start = (bf16[256,4096]{1,0:T(8,128)(2,1)S(1)}, bf16[256,4096]{1,0:T(8,128)(2,1)}, u32[]{:S(2)}) copy-start(bf16[256,4096]{1,0:T(8,128)(2,1)} %param.16) | copy-start | bytes 6291460
  8.4 5.8 %copy-start.4 = (bf16[1024,1024]{1,0:T(8,128)(2,1)S(1)}, bf16[1024,1024]{1,0:T(8,128)(2,1)}, u32[]{:S(2)}) copy-start(bf16[1024,1024]{1,0:T(8,128)(2,1)} %param.15) | copy-start | bytes 6291460
  17.7 24.9 %copy-start.10 = (s32[128,2,1]{0,2,1:T(1,128)S(1)}, s32[128,2,1]{0,2,1:T(1,128)}, u32[]{:S(2)}) copy-start(s32[128,2,1]{0,2,1:T(1,128)} %param.17) | copy-start | bytes 3076
  34.1 42.8 %copy-start.6 = (bf16[128,4096]{1,0:T(8,128)(2,1)S(1)}, bf16[128,4096]{1,0:T(8,128)(2,1)}, u32[]{:S(2)}) copy-start(bf16[128,4096]{1,0:T(8,128)(2,1)} %param.13) | copy-start | bytes 3145732
  43.0 0.6 copy-start.9
  48.8 21.4 %all-to-all-start.3 = ((bf16[16,2,512]{2,1,0:T(2,128)(2,1)}), bf16[16,2,512]{2,1,0:T(2,128)(2,1)S(1)}, u32[]{:S(2)}, u32[]{:S(2)}) async-start(bf16[16,2,512]{2,1,0:T(2,128)(2,1)} %reshape.169), calls=%async_computation.4 | async-start | bytes 65536 | tf_op jit(solution)/shard_map/all_to_all | solution.py:113
  70.3 13.3 %all-to-all-start = ((s32[16,1,1024]{2,1,0:T(1,128)}), s32[16,1,1024]{2,1,0:T(1,128)}, u32[]{:S(2)}, u32[]{:S(2)}) async-start(s32[16,1,1024]{2,1,0:T(1,128)} %reshape.171), calls=%async_computation | async-start | bytes 131072 | tf_op jit(solution)/shard_map/all_to_all | solution.py:106
  83.6 55.1 %all-to-all-start.1 = ((bf16[16,32,4096]{2,1,0:T(8,128)(2,1)}), bf16[16,32,4096]{2,1,0:T(8,128)(2,1)}, u32[]{:S(2)}, u32[]{:S(2)}) async-start(bf16[16,32,4096]{2,1,0:T(8,128)(2,1)} %bitcast.123), calls=%async_computation.1 | async-start | bytes 8388608 | tf_op jit(solution)/shard_map/all_to_all | solution.py:99
  138.7 3.6 copy-start.8
  138.7 21.2 %copy-start.2 = (bf16[128,4096]{1,0:T(8,128)(2,1)S(1)}, bf16[128,4096]{1,0:T(8,128)(2,1)}, u32[]{:S(2)}) copy-start(bf16[128,4096]{1,0:T(8,128)(2,1)} %param.12) | copy-start | bytes 3145732
  154.1 11.8 %all-to-all-start.2 = ((f32[16,1,1024]{2,1,0:T(1,128)}), f32[16,1,1024]{2,1,0:T(1,128)S(1)}, u32[]{:S(2)}, u32[]{:S(2)}) async-start(f32[16,1,1024]{2,1,0:T(1,128)} %reshape.173), calls=%async_computation.2 | async-start | bytes 131072 | tf_op jit(solution)/shard_map/all_to_all | solution.py:136
  159.4 184.9 %reduce-scatter.2.cloned.1.call-start = ((), (), s32[]{:S(2)}) async-start(), calls=%async_computation.5 | async-start | bytes 22282240 | tf_op jit(solution)/shard_map/reduce_scatter | solution.py:180
  185.4 1.0 copy-start.7
  196.0 1.2 copy-start.3
  208.8 0.9 copy-start.5
  208.9 205.4 %all-reduce.3.cloned.1.call-start = ((), (), s32[]{:S(2)}) async-start(), calls=%async_computation.6 | async-start | bytes 2621440 | tf_op jit(solution)/shard_map/psum | solution.py:192
  406.8 11.4 %copy-start.1 = (bf16[256,4096]{1,0:T(8,128)(2,1)S(1)}, bf16[256,4096]{1,0:T(8,128)(2,1)}, u32[]{:S(2)}) copy-start(bf16[256,4096]{1,0:T(8,128)(2,1)} %param.16) | copy-start | bytes 6291460
Sparse Core Ops, SparseCore 0:
  209.0 135.3 reduce-scatter.1
  346.7 64.7 all-reduce.2
where the time goes:
time: 428 us; the launch traced here: 425 us
  waiting for transfers between devices  184 us (43%)
  blocking collectives  62.4 us (15%)
  other arithmetic  54.8 us (13%)
  local copies, waits for them, and re-layouts  46.2 us (11%)
  matrix products  39 us (9%)
  starting transfers between devices  24.4 us (6%)
  between operations  14.3 us (3%)
    reduce_scatter x1, waiting for transfers between devices, on_device(): lax.psum_scatter(grad_term(input_blocks, grad_blocks, query_grad, query_b...  129 us
    psum x1, blocking collectives, on_device(): local_sum, table_sum = lax.psum((local, table_part), 'rep')  62.4 us
    all_to_all x1, waiting for transfers between devices, on_device(): lax.all_to_all(payload.reshape(shards, capacity, model_width), 'tab', spl...  46.5 us
    reduce_sum x2, other arithmetic, place_block(): return jnp.sum(jnp.where(equal, block_spread[:, :, :, None], 0.0), axis=2)  16.5 us
    unnamed x32, local copies, waits for them, and re-layouts  11.1 us
    reduce_sum x2, other arithmetic, pick_block(): return jnp.sum(jnp.where(equal, block_scores[:, :, None, :], 0.0), axis=3)  11.1 us
    reduce_sum x1, other arithmetic, on_device(): jnp.sum(jnp.where(matches, arrived_weights[:, :, None].astype(jnp.float32...  10.9 us
    concatenate x1, other arithmetic, grad_term(): joined = jnp.concatenate([weight_part, key_part], axis=1)  9.21 us
  transfers between devices with their start and end apart: 6, of which 4 were waited for; matrix products, arithmetic and copies ran while one was open for 8% of the time, Pallas kernels for 0%

commit v1 on v0

v1 whole, which is shorter than its diff:
```python
import functools

import jax
import jax.numpy as jnp
from jax import lax
from jax.experimental import pallas as pl
from jax.experimental.pallas import tpu as pltpu
from jax.sharding import PartitionSpec as P

BF = jnp.bfloat16
F32 = jnp.float32
I32 = jnp.int32


def dot_nn(a, b):
    return lax.dot_general(a, b, (((1,), (0,)), ((), ())), preferred_element_type=F32)


def dot_nt(a, b):
    return lax.dot_general(a, b, (((1,), (1,)), ((), ())), preferred_element_type=F32)


def dot_tn(a, b):
    return lax.dot_general(a, b, (((0,), (0,)), ((), ())), preferred_element_type=F32)


def three(x):
    a = x.astype(BF)
    rest = x - a.astype(F32)
    b = rest.astype(BF)
    c = (rest - b.astype(F32)).astype(BF)
    return a, b, c


def iota(shape, dim):
    return lax.broadcasted_iota(I32, shape, dim)


def dispatch_kernel(capacity, own_row, own_col, grad, rows, payload, slot_row):
    messages = own_row.shape[1]
    tokens = grad.shape[0]
    slots, wide = payload.shape
    width = grad.shape[1]
    same = own_row[...] == own_col[...]
    earlier = iota((messages, messages), 0) < iota((messages, messages), 1)
    rank = jnp.sum(jnp.where(same & earlier, 1, 0), axis=0, keepdims=True)
    place = own_row[...] * capacity + rank
    slot_row[...] = place
    hit = jnp.where(iota((slots, messages), 0) == place, 1.0, 0.0)
    either = hit[:, :tokens]
    for head in range(1, messages // tokens):
        either = either + hit[:, head * tokens : (head + 1) * tokens]
    either = either.astype(BF)
    step = 512
    for at in range(0, width, step):
        payload[:, at : at + step] = dot_nn(either, grad[:, at : at + step]).astype(BF)
    payload[:, width:] = dot_nn(hit.astype(BF), rows[...]).astype(BF)


def score_kernel(
    heads, inputs, weight, keys, picks, slot_col, low_out, weights_out, send_out, acc
):
    step = pl.program_id(0)

    @pl.when(step == 0)
    def _():
        acc[...] = jnp.zeros_like(acc)

    acc[...] += dot_nn(inputs[...], weight[...])

    @pl.when(step == pl.num_programs(0) - 1)
    def _():
        tokens, cols = acc.shape
        lanes = picks.shape[1]
        blocks = 2 * heads
        half = cols // blocks
        count = keys.shape[0]
        low_out[...] = acc[...].astype(BF)
        pick = picks[...]
        low = pick % 128
        high = pick // 128
        lane_block = iota((tokens, lanes), 1) // (lanes // blocks)
        chosen = jnp.zeros((tokens, lanes), F32)
        for b in range(blocks):
            parts = three(acc[:, b * half : (b + 1) * half])
            block_keys = keys[:, b * half : (b + 1) * half]
            for j in range(count // 128):
                rows = block_keys[j * 128 : (j + 1) * 128]
                score = dot_nt(parts[2], rows) + dot_nt(parts[1], rows) + dot_nt(parts[0], rows)
                got = jnp.take_along_axis(score, low, axis=1)
                chosen = jnp.where((high == j) & (lane_block == b), got, chosen)
        top = lanes // blocks
        even = lane_block % 2 == 0
        other = jnp.where(
            even, pltpu.roll(chosen, lanes - top, axis=1), pltpu.roll(chosen, top, axis=1)
        )
        scores = chosen + other
        head_of = lane_block // 2
        peak = jnp.zeros((tokens, lanes), F32)
        for h in range(heads):
            most = jnp.max(jnp.where(head_of == h, scores, -jnp.inf), axis=1, keepdims=True)
            peak = jnp.where(head_of == h, most, peak)
        raised = jnp.exp(scores - peak)
        total = jnp.zeros((tokens, lanes), F32)
        for h in range(heads):
            part = jnp.sum(jnp.where(head_of == h, raised, 0.0), axis=1, keepdims=True)
            total = jnp.where(head_of == h, part * 0.5, total)
        soft = raised / total
        weights_out[...] = soft
        slots = send_out.shape[0]
        low_soft = soft.astype(BF).astype(F32)
        sent = jnp.zeros((slots, lanes), F32)
        for h in range(heads):
            hit = jnp.where(
                iota((tokens, slots), 1) == slot_col[h * tokens : (h + 1) * tokens], 1.0, 0.0
            ).astype(BF)
            turned = low_soft if h == 0 else pltpu.roll(low_soft, lanes - h * 2 * top, axis=1)
            sent = sent + dot_tn(hit, turned.astype(BF))
        send_out[...] = sent.astype(BF)


def shard_kernel(width, arrived, values, back):
    product = dot_nt(arrived[:, :width], values[...])
    pick = arrived[:, width:].astype(I32)
    out = jnp.zeros(pick.shape, F32)
    for j in range(values.shape[0] // 128):
        got = jnp.take_along_axis(product[:, j * 128 : (j + 1) * 128], pick % 128, axis=1)
        out = jnp.where(pick // 128 == j, got, out)
    back[...] = out


def table_kernel(top, arrived, rows, soft, part, spread):
    @pl.when(pl.program_id(0) == 0)
    def _():
        count, slots = spread.shape
        row_t = rows[...].astype(F32).T
        soft_t = soft[...].astype(F32).T
        for at in range(0, slots, 128):
            names = iota((count, 128), 0).astype(F32)
            held = jnp.zeros((count, 128), F32)
            for k in range(top):
                held = held + jnp.where(
                    names == row_t[k : k + 1, at : at + 128], soft_t[k : k + 1, at : at + 128], 0.0
                )
            spread[:, at : at + 128] = held.astype(BF)

    part[...] = dot_nn(spread[...], arrived[...]).astype(BF)


def grad_kernel(heads, returned, slot_col, soft, picks, keys, half_out, query_out, placed):
    tokens, lanes = soft.shape
    blocks = 2 * heads
    top = lanes // blocks
    slots = returned.shape[0]
    head_of = iota((tokens, lanes), 1) // (2 * top)
    parts = three(returned[...])
    slot_grad = jnp.zeros((tokens, lanes), F32)
    for h in range(heads):
        hit = jnp.where(
            iota((tokens, slots), 1) == slot_col[h * tokens : (h + 1) * tokens], 1.0, 0.0
        ).astype(BF)
        got = dot_nn(hit, parts[2]) + dot_nn(hit, parts[1]) + dot_nn(hit, parts[0])
        slot_grad = jnp.where(head_of == h, got, slot_grad)
    weights = soft[...]
    scaled = weights * slot_grad
    mean = jnp.zeros((tokens, lanes), F32)
    for h in range(heads):
        part = jnp.sum(jnp.where(head_of == h, scaled, 0.0), axis=1, keepdims=True)
        mean = jnp.where(head_of == h, part * 0.5, mean)
    score_grad = weights * (slot_grad - mean)
    count = keys.shape[0]
    tiles = count // 128
    pick = picks[...]
    low = pick % 128
    high = pick // 128 + tiles * (iota((tokens, lanes), 1) // top)
    for t in range(tokens):
        left = jnp.where(
            iota((blocks * tiles, lanes), 0) == high[t : t + 1], score_grad[t : t + 1], 0.0
        ).astype(BF)
        right = jnp.where(iota((128, lanes), 0) == low[t : t + 1], 1.0, 0.0).astype(BF)
        placed[t] = dot_nt(left, right)
    half = query_out.shape[1] // blocks
    quarter = half_out.shape[2]
    each = quarter // 128
    for b in range(blocks):
        total = jnp.zeros((tokens, half), F32)
        for q in range(count // quarter):
            for i in range(each):
                row = b * tiles + q * each + i
                sums = placed[:, row, :].astype(BF)
                half_out[q * blocks + b, :, i * 128 : (i + 1) * 128] = sums
                at = (q * each + i) * 128
                total = total + dot_nn(sums, keys[at : at + 128, b * half : (b + 1) * half])
        query_out[:, b * half : (b + 1) * half] = total.astype(BF)


VM = pl.BlockSpec(memory_space=pltpu.VMEM)
LIMIT = 56 * 1024 * 1024


def local(body, out_shape, **more):
    return pl.pallas_call(
        body,
        out_shape=out_shape,
        compiler_params=pltpu.CompilerParams(vmem_limit_bytes=LIMIT),
        **more,
    )


def sds(shape, dtype):
    return jax.ShapeDtypeStruct(shape, dtype)


def on_device(inputs, grad_out, query_weight, sub_keys, values, owner, slot_rows, sub_index):
    tokens, width = inputs.shape
    cols = query_weight.shape[1]
    count = sub_keys.shape[0]
    heads, top = slot_rows.shape[1:]
    blocks = 2 * heads
    lanes = blocks * top
    shards = lax.axis_size("tab")
    groups = lax.axis_size("rep")
    messages = tokens * heads
    capacity = 2 * messages // shards
    slots = shards * capacity
    table_rows = values.shape[0]
    across = functools.partial(lax.all_to_all, axis_name="tab", tiled=True)

    own_row = owner.reshape(tokens, heads).T.reshape(1, messages)
    own_col = own_row.reshape(messages, 1)
    rows4 = jnp.tile(jnp.transpose(slot_rows, (1, 0, 2)).reshape(messages, top), (1, blocks))
    payload, slot_row = local(
        functools.partial(dispatch_kernel, capacity),
        (sds((slots, width + lanes), BF), sds((1, messages), I32)),
        name="dispatch",
    )(own_row, own_col, grad_out, rows4.astype(BF))
    arrived = across(
        payload.reshape(shards, capacity, width + lanes), split_axis=0, concat_axis=0
    ).reshape(slots, width + lanes)
    slot_col = slot_row.reshape(messages, 1)
    picks = sub_index.reshape(tokens, lanes)

    depth = 512
    low_query, weights, send_weights = local(
        functools.partial(score_kernel, heads),
        (sds((tokens, cols), BF), sds((tokens, lanes), F32), sds((slots, lanes), BF)),
        grid=(width // depth,),
        in_specs=[
            pl.BlockSpec((tokens, depth), lambda i: (0, i)),
            pl.BlockSpec((depth, cols), lambda i: (i, 0)),
            pl.BlockSpec((count, cols), lambda i: (0, 0)),
            pl.BlockSpec((tokens, lanes), lambda i: (0, 0)),
            pl.BlockSpec((messages, 1), lambda i: (0, 0)),
        ],
        out_specs=(
            pl.BlockSpec((tokens, cols), lambda i: (0, 0)),
            pl.BlockSpec((tokens, lanes), lambda i: (0, 0)),
            pl.BlockSpec((slots, lanes), lambda i: (0, 0)),
        ),
        scratch_shapes=[pltpu.VMEM((tokens, cols), F32)],
        name="scores",
    )(inputs, query_weight, sub_keys, picks, slot_col)

    back = local(
        functools.partial(shard_kernel, width),
        sds((slots, lanes), F32),
        grid=(slots // 128,),
        in_specs=[
            pl.BlockSpec((128, width + lanes), lambda i: (i, 0)),
            pl.BlockSpec((table_rows, width), lambda i: (0, 0)),
        ],
        out_specs=pl.BlockSpec((128, lanes), lambda i: (i, 0)),
        name="shard",
    )(arrived, values)
    returned = across(back.reshape(shards, capacity, lanes), split_axis=0, concat_axis=0)
    returned = returned.reshape(slots, lanes)

    arrived_weights = across(
        send_weights.reshape(shards, capacity, lanes), split_axis=0, concat_axis=0
    ).reshape(slots, lanes)
    table_part = local(
        functools.partial(table_kernel, top),
        sds((table_rows, width), BF),
        grid=(width // 512,),
        in_specs=[
            pl.BlockSpec((slots, 512), lambda i: (0, i)),
            pl.BlockSpec((slots, lanes), lambda i: (0, width // lanes)),
            pl.BlockSpec((slots, lanes), lambda i: (0, 0)),
        ],
        out_specs=pl.BlockSpec((table_rows, 512), lambda i: (0, i)),
        scratch_shapes=[pltpu.VMEM((table_rows, slots), BF)],
        name="table",
    )(arrived, arrived, arrived_weights)
    table_pieces = lax.all_to_all(
        table_part.reshape(groups, table_rows // groups, width), "rep", 0, 0, tiled=True
    )
    table_piece = jnp.sum(table_pieces.astype(F32), axis=0).astype(BF)
    table_grad = lax.all_gather(table_piece, "rep", axis=0, tiled=True)

    quarters = shards // blocks
    quarter = count // quarters
    half_grad, query_grad = local(
        functools.partial(grad_kernel, heads),
        (sds((shards, tokens, quarter), BF), sds((tokens, cols), BF)),
        scratch_shapes=[pltpu.VMEM((tokens, blocks * count // 128, 128), F32)],
        name="grads",
    )(returned, slot_col, weights, picks, sub_keys)
    input_grad = lax.dot_general(
        query_grad, query_weight, (((1,), (1,)), ((), ())), preferred_element_type=F32
    ).astype(BF)

    weight_rows = width // shards
    half = cols // blocks
    early = jnp.concatenate(
        [
            jnp.transpose(inputs.reshape(tokens, shards, weight_rows), (1, 0, 2)),
            jnp.tile(jnp.transpose(low_query.reshape(tokens, blocks, half), (1, 0, 2)), (quarters, 1, 1)),
        ],
        axis=2,
    )
    early = across(early, split_axis=0, concat_axis=0).reshape(shards * tokens, weight_rows + half)
    group_inputs = early[:, :weight_rows]
    group_query = early[:, weight_rows:]
    group_half = across(half_grad, split_axis=0, concat_axis=0).reshape(shards * tokens, quarter)
    group_grad = lax.all_gather(query_grad, "tab", axis=0, tiled=True)
    weight_part = dot_tn(group_inputs, group_grad)
    key_part = dot_tn(group_half, group_query)
    key_rows = count // shards
    members = [[q * blocks + b for b in range(blocks)] for q in range(quarters)]
    key_part = lax.all_to_all(
        key_part.reshape(blocks, key_rows, half), "tab", 0, 0, axis_index_groups=members, tiled=True
    )
    key_part = jnp.transpose(key_part, (1, 0, 2)).reshape(key_rows, cols)
    weight_grad, key_grad = lax.psum((weight_part, key_part), "rep")
    return (input_grad, weight_grad, key_grad, table_grad)


def solution(mesh):
    placed = (
        P(("rep", "tab"), None),
        P(("rep", "tab"), None),
        P(),
        P(),
        P("tab", None),
        P(("rep", "tab"), None, None),
        P(("rep", "tab"), None, None),
        P(("rep", "tab"), None, None, None),
    )
    return jax.shard_map(
        on_device,
        mesh=mesh,
        in_specs=placed,
        out_specs=(P(("rep", "tab"), None), P("tab", None), P("tab", None), P("tab", None)),
        check_vma=False,
    )
```

time: 428 us -> 305 us (0.71)
  waiting for transfers between devices: 184 us -> 93.4 us
  blocking collectives: 62.4 us -> 116 us
  other arithmetic: 54.8 us -> 3.31 us
  Pallas kernels: 0 us -> 39.1 us
  local copies, waits for them, and re-layouts: 46.2 us -> 12.4 us
  matrix products: 39 us -> 12.2 us
  starting transfers between devices: 24.4 us -> 12 us
    reduce_scatter x1 -> x0, waiting for transfers between devices: 129 us -> none  [on_device(): lax.psum_scatter(grad_term(input_blocks, grad_blocks, query_grad, query_b...]
    all_to_all x0 -> x4, blocking collectives: none -> 116 us  [the longest x1 59.3 us: on_device(): across(payload.reshape(shards, capacity, width + lanes), split_axis=0, co...]
    psum x1 -> x0, blocking collectives: 62.4 us -> none  [on_device(): local_sum, table_sum = lax.psum((local, table_part), 'rep')]
    psum x1, waiting for transfers between devices: 0.01 us -> 57.1 us  [on_device(): weight_grad, key_grad = lax.psum((weight_part, key_part), 'rep')]
    pallas_call x0 -> x5, Pallas kernels: none -> 39.1 us  [the longest x1 11.2 us: on_device(): local(functools.partial(score_kernel, heads), (sds((tokens, cols), BF), s...]
    reduce_sum x6 -> x1, other arithmetic: 38.6 us -> 1.04 us  [on_device(): table_piece = jnp.sum(table_pieces.astype(F32), axis=0).astype(BF)]
    dot_general x11 -> x2, matrix products: 30 us -> 4.91 us  [dot_tn(): lax.dot_general(a, b, (((0,), (0,)), ((), ())), preferred_element_type=F32)]
    all_to_all x4 -> x3, waiting for transfers between devices: 54.6 us -> 36.2 us  [the longest x1 23.8 us: on_device(): across(early, split_axis=0, concat_axis=0)]
  transfers between devices with their start and end apart: 6 -> 6, of which waited for: 4 -> 3; matrix products, arithmetic and copies ran while one was open for 8% -> 6% of each run, Pallas kernels for 0% -> 7%
where the time goes in v1:
time: 305 us; the launch traced here: 302 us
  blocking collectives  116 us (38%)
  waiting for transfers between devices  93.4 us (31%)
  Pallas kernels  39.1 us (13%)
  between operations  13.9 us (5%)
  local copies, waits for them, and re-layouts  12.4 us (4%)
  matrix products  12.2 us (4%)
  starting transfers between devices  12 us (4%)
  other arithmetic  3.31 us (1%)
    all_to_all x1, blocking collectives, on_device(): across(payload.reshape(shards, capacity, width + lanes), split_axis=0, co...  59.3 us
    psum x1, waiting for transfers between devices, on_device(): weight_grad, key_grad = lax.psum((weight_part, key_part), 'rep')  57.1 us
    all_to_all x1, blocking collectives, on_device(): lax.all_to_all(table_part.reshape(groups, table_rows // groups, width), '...  35.6 us
    all_to_all x1, waiting for transfers between devices, on_device(): across(early, split_axis=0, concat_axis=0)  23.8 us
    all_to_all x1, blocking collectives, on_device(): across(send_weights.reshape(shards, capacity, lanes), split_axis=0, conca...  13.3 us
    all_to_all x1, waiting for transfers between devices, on_device(): across(half_grad, split_axis=0, concat_axis=0)  12.4 us
    pallas_call x1, Pallas kernels, on_device(): local(functools.partial(score_kernel, heads), (sds((tokens, cols), BF), s...  11.2 us
    pallas_call x1, Pallas kernels, on_device(): local(functools.partial(table_kernel, top), sds((table_rows, width), BF),...  9.21 us
  transfers between devices with their start and end apart: 6, of which 3 were waited for; matrix products, arithmetic and copies ran while one was open for 6% of the time, Pallas kernels for 7%

profile of v1, /device:TPU:1, one launch (start us, length us, event | category | flops | bytes accessed | tf_op | source)
XLA Modules:
  0.0 302.3 jit_solution(14853515757240322321)
XLA Ops:
  7.2 0.8 copy_bitcast_fusion
  7.9 0.7 copy.18.rows
  8.7 1.5 copy.17.own_col
  10.1 4.8 %dispatch.1 = (bf16[512,4224]{1,0:T(8,128)(2,1)}, s32[1,256]{1,0:T(1,128)}) custom-call(s32[1,256]{1,0:T(1,128)} %bitcast.68, s32[256,1]{1,0:T(8,128)} %copy.17.own_col, bf16[128,4096]{1,0:T(8,128)(2,1)} %grad.1, bf16[256,128]{1,0:T(8,128)(2,1)} %copy.18.rows), custom_call_target="tpu_custom_call" | custom-call | tf_op jit(solution)/shard_map/dispatch/pallas_call | solution.py:232
  15.0 59.3 %all_to_all.35 = bf16[16,32,4224]{2,1,0:T(8,128)(2,1)} all-to-all(bf16[16,32,4224]{2,1,0:T(8,128)(2,1)} %bitcast.51), channel_id=1, replica_groups=mesh['rep'=8,'tab'=16] {'tab'}, dimensions={0} | all-to-all | bytes 8650752 | tf_op jit(solution)/shard_map/all_to_all | solution.py:237
  74.2 6.8 %shard.1 = f32[512,128]{1,0:T(8,128)} custom-call(bf16[512,4224]{1,0:T(8,128)(2,1)} %bitcast.47, bf16[256,4096]{1,0:T(8,128)(2,1)} %values.1), custom_call_target="tpu_custom_call" | custom-call | tf_op jit(solution)/shard_map/shard/pallas_call | solution.py:264
  81.0 3.6 %all-to-all-start.1 = ((f32[16,32,128]{2,1,0:T(8,128)}), f32[16,32,128]{2,1,0:T(8,128)S(1)}, u32[]{:S(2)}, u32[]{:S(2)}) async-start(f32[16,32,128]{2,1,0:T(8,128)} %bitcast.59), calls=%async_computation.1 | async-start | bytes 524288 | tf_op jit(solution)/shard_map/all_to_all | solution.py:275
  84.6 0.7 copy.19.picks
  85.4 0.8 copy.21.slot_col
  86.2 11.2 %scores.1 = (bf16[128,1024]{1,0:T(8,128)(2,1)}, f32[128,128]{1,0:T(8,128)}, bf16[512,128]{1,0:T(8,128)(2,1)}) custom-call(bf16[128,4096]{1,0:T(8,128)(2,1)} %inputs.1, bf16[4096,1024]{1,0:T(8,128)(2,1)} %weight.1, bf16[1024,1024]{1,0:T(8,128)(2,1)} %keys.3, s32[128,128]{1,0:T(8,128)} %copy.19.picks, s32[256,1]{1,0:T(8,128)} %copy.21.slot_col), custom_call_target="tpu_custom_call" | custom-call | tf_op jit(solution)/shard_map/scores/pallas_call | solution.py:244
  97.3 0.7 copy-done.3
  98.0 7.1 %grads.1 = (bf16[16,128,256]{2,1,0:T(8,128)(2,1)}, bf16[128,1024]{1,0:T(8,128)(2,1)}) custom-call(f32[512,128]{1,0:T(8,128)} %bitcast.58, s32[256,1]{1,0:T(8,128)} %copy.21.slot_col, f32[128,128]{1,0:T(8,128)} %get-tuple-element.13.soft, s32[128,128]{1,0:T(8,128)} %copy.19.picks, bf16[1024,1024]{1,0:T(8,128)(2,1)} %keys.3), custom_call_target="tpu_custom_call" | custom-call | tf_op jit(solution)/shard_map/grads/pallas_call | solution.py:302
  105.2 13.3 %all_to_all.36 = bf16[16,32,128]{2,1,0:T(8,128)(2,1)} all-to-all(bf16[16,32,128]{2,1,0:T(8,128)(2,1)S(1)} %bitcast.65), channel_id=1, replica_groups=mesh['rep'=8,'tab'=16] {'tab'}, dimensions={0} | all-to-all | bytes 262144 | tf_op jit(solution)/shard_map/all_to_all | solution.py:278
  118.4 9.2 %table.1 = bf16[256,4096]{1,0:T(8,128)(2,1)} custom-call(bf16[512,4224]{1,0:T(8,128)(2,1)} %bitcast.48, bf16[512,4224]{1,0:T(8,128)(2,1)} %bitcast.49, bf16[512,128]{1,0:T(8,128)(2,1)} %bitcast.63), custom_call_target="tpu_custom_call" | custom-call | tf_op jit(solution)/shard_map/table/pallas_call | solution.py:281
  127.6 35.6 %all_to_all.37 = bf16[8,32,4096]{2,1,0:T(8,128)(2,1)S(1)} all-to-all(bf16[8,32,4096]{2,1,0:T(8,128)(2,1)} %bitcast.50), channel_id=1, replica_groups=mesh['rep'=8,'tab'=16] {'rep'}, dimensions={0} | all-to-all | bytes 4194304 | tf_op jit(solution)/shard_map/all_to_all | solution.py:294
  163.2 4.5 %all-to-all-start.3 = ((bf16[16,128,256]{2,1,0:T(8,128)(2,1)}), bf16[16,128,256]{2,1,0:T(8,128)(2,1)}, u32[]{:S(2)}, u32[]{:S(2)}) async-start(bf16[16,128,256]{2,1,0:T(8,128)(2,1)} %get-tuple-element.16), calls=%async_computation.3 | async-start | bytes 2097152 | tf_op jit(solution)/shard_map/all_to_all | solution.py:324
  167.8 1.0 reduce_sum.12
  169.0 0.2 reshape.77
  169.3 1.5 pad_maximum_fusion
  170.8 12.4 %all-to-all-done.3 = bf16[16,128,256]{2,1,0:T(8,128)(2,1)} async-done(((bf16[16,128,256]{2,1,0:T(8,128)(2,1)}), bf16[16,128,256]{2,1,0:T(8,128)(2,1)}, u32[]{:S(2)}, u32[]{:S(2)}) %all-to-all-start.3) | async-done | bytes 1048608 | tf_op jit(solution)/shard_map/all_to_all | solution.py:324
  183.2 3.9 %all-to-all-start.2 = ((bf16[16,128,512]{2,1,0:T(8,128)(2,1)}), bf16[16,128,512]{2,1,0:T(8,128)(2,1)S(1)}, u32[]{:S(2)}, u32[]{:S(2)}) async-start(bf16[16,128,512]{2,1,0:T(8,128)(2,1)} %pad_maximum_fusion), calls=%async_computation.2 | async-start | bytes 4194304 | tf_op jit(solution)/shard_map/all_to_all | solution.py:321
  187.2 1.5 copy.25
  188.7 23.8 %all-to-all-done.2 = bf16[16,128,512]{2,1,0:T(8,128)(2,1)S(1)} async-done(((bf16[16,128,512]{2,1,0:T(8,128)(2,1)}), bf16[16,128,512]{2,1,0:T(8,128)(2,1)S(1)}, u32[]{:S(2)}, u32[]{:S(2)}) %all-to-all-start.2) | async-done | bytes 2097184 | tf_op jit(solution)/shard_map/all_to_all | solution.py:321
  212.5 0.4 fusion
  212.9 7.9 %all_to_all.38 = f32[4,64,256]{2,1,0:T(8,128)S(1)} all-to-all(f32[4,64,256]{2,1,0:T(8,128)S(1)} %fusion), channel_id=1, replica_groups={{0,1,2,3},{4,5,6,7},{8,9,10,11},{12,13,14,15},{16,17,18,19},{20,21,22,2..., dimensions={0} | all-to-all | bytes 524288 | tf_op jit(solution)/shard_map/all_to_all | solution.py:330
  220.8 0.7 copy.29
  221.6 4.5 %fusion.1 = f32[256,1024]{1,0:T(8,128)} fusion(bf16[2048,1024]{1,0:T(8,128)(2,1)} %all-gather.3.cloned.1.call-done, bf16[2048,512]{1,0:T(8,128)(2,1)S(1)} %bitcast.56), kind=kOutput, calls=%fused_computation.5 | convolution fusion | flops 1073741824 | bytes 6291456 | tf_op jit(solution)/shard_map/dot_general | solution.py:24
  226.1 7.2 %convolution_convert_fusion = bf16[128,4096]{1,0:T(8,128)(2,1)} fusion(bf16[128,1024]{1,0:T(8,128)(2,1)S(1)} %copy-done.2, bf16[4096,1024]{1,0:T(8,128)(2,1)} %weight.1), kind=kOutput, calls=%fused_computation | convolution fusion | flops 1074266112 | bytes 9699328 | tf_op jit(solution)/shard_map/dot_general | solution.py:308
  233.3 57.1 %all-reduce.3.cloned.1.call-done = (f32[256,1024]{1,0:T(8,128)}, f32[64,1024]{1,0:T(8,128)}) async-done(((f32[256,1024]{1,0:T(8,128)}, f32[64,1024]{1,0:T(8,128)}), (f32[256,1024]{1,0:T(8,128)}, f32[64,1024]{1,0:T(8,128)})) %all-reduce.3.cloned.1.call-update) | async-done | bytes 1310736 | tf_op jit(solution)/shard_map/psum | solution.py:334
  290.4 2.3 copy.36
  292.7 1.7 copy.37
  294.4 1.3 copy.38
  (28 shorter events, 0.4 us)
Async XLA Ops:
  74.2 10.4 %copy-start.6 = (s32[128,2,2,32]{0,3,2,1:T(8,128)S(1)}, s32[128,2,2,32]{0,3,2,1:T(8,128)}, u32[]{:S(2)}) copy-start(s32[128,2,2,32]{0,3,2,1:T(8,128)} %param.15) | copy-start | bytes 196612
  74.2 11.1 %copy-start.7 = (s32[1,256]{1,0:T(1,128)S(1)}, s32[1,256]{1,0:T(1,128)}, u32[]{:S(2)}) copy-start(s32[1,256]{1,0:T(1,128)} %get-tuple-element.12) | copy-start | bytes 3076
  81.0 16.3 %all-to-all-start.1 = ((f32[16,32,128]{2,1,0:T(8,128)}), f32[16,32,128]{2,1,0:T(8,128)S(1)}, u32[]{:S(2)}, u32[]{:S(2)}) async-start(f32[16,32,128]{2,1,0:T(8,128)} %bitcast.59), calls=%async_computation.1 | async-start | bytes 524288 | tf_op jit(solution)/shard_map/all_to_all | solution.py:275
  84.6 137.0 %all-gather.3.cloned.1.call-start = ((), (), s32[]{:S(2)}) async-start(), calls=%async_computation.7 | async-start | bytes 4456448 | tf_op jit(solution)/shard_map/all_gather | solution.py:325
  97.3 7.8 %copy-start.5 = (bf16[512,128]{1,0:T(8,128)(2,1)S(1)}, bf16[512,128]{1,0:T(8,128)(2,1)}, u32[]{:S(2)}) copy-start(bf16[512,128]{1,0:T(8,128)(2,1)} %get-tuple-element.17) | copy-start | bytes 393220
  97.3 0.7 copy-start.3
  163.2 5.6 %copy-start = (bf16[128,4096]{1,0:T(8,128)(2,1)S(1)}, bf16[128,4096]{1,0:T(8,128)(2,1)}, u32[]{:S(2)}) copy-start(bf16[128,4096]{1,0:T(8,128)(2,1)} %inputs.1) | copy-start | bytes 3145732
  163.2 20.0 %all-to-all-start.3 = ((bf16[16,128,256]{2,1,0:T(8,128)(2,1)}), bf16[16,128,256]{2,1,0:T(8,128)(2,1)}, u32[]{:S(2)}, u32[]{:S(2)}) async-start(bf16[16,128,256]{2,1,0:T(8,128)(2,1)} %get-tuple-element.16), calls=%async_computation.3 | async-start | bytes 2097152 | tf_op jit(solution)/shard_map/all_to_all | solution.py:324
  167.7 1.2 copy-start.4
  167.7 65.6 %all-gather.5.cloned.1.call-start = ((), (), s32[]{:S(2)}) async-start(), calls=%async_computation.8 | async-start | bytes 2359296 | tf_op jit(solution)/shard_map/all_gather | solution.py:298
  183.2 29.2 %all-to-all-start.2 = ((bf16[16,128,512]{2,1,0:T(8,128)(2,1)}), bf16[16,128,512]{2,1,0:T(8,128)(2,1)S(1)}, u32[]{:S(2)}, u32[]{:S(2)}) async-start(bf16[16,128,512]{2,1,0:T(8,128)(2,1)} %pad_maximum_fusion), calls=%async_computation.2 | async-start | bytes 4194304 | tf_op jit(solution)/shard_map/all_to_all | solution.py:321
  187.1 103.3 %all-reduce.3.cloned.1.call-start = ((), (), s32[]{:S(2)}) async-start(), calls=%async_computation.9 | async-start | bytes 2621440 | tf_op jit(solution)/shard_map/psum | solution.py:334
  221.5 4.5 %copy-start.2 = (bf16[128,1024]{1,0:T(8,128)(2,1)S(1)}, bf16[128,1024]{1,0:T(8,128)(2,1)}, u32[]{:S(2)}) copy-start(bf16[128,1024]{1,0:T(8,128)(2,1)} %get-tuple-element.14) | copy-start | bytes 786436
  233.3 61.1 %copy-start.1 = (bf16[256,4096]{1,0:T(8,128)(2,1)S(1)}, bf16[256,4096]{1,0:T(8,128)(2,1)}, u32[]{:S(2)}) copy-start(bf16[256,4096]{1,0:T(8,128)(2,1)} %all-gather.5.cloned.1.call-done) | copy-start | bytes 6291460
Sparse Core Ops, SparseCore 0:
  105.3 55.4 all-gather.2
  170.3 25.6 all-gather.4
  226.2 64.2 all-reduce.2

commit v2 on v1

--- a/solution.py
+++ b/solution.py
@@ -119,7 +119,7 @@
         send_out[...] = sent.astype(BF)
 
 
-def shard_kernel(width, arrived, values, back):
+def shard_kernel(width, arrived, values, after, back):
     product = dot_nt(arrived[:, :width], values[...])
     pick = arrived[:, width:].astype(I32)
     out = jnp.zeros(pick.shape, F32)
@@ -198,10 +198,13 @@
 LIMIT = 56 * 1024 * 1024
 
 
-def local(body, out_shape, **more):
+def local(body, out_shape, micros, **more):
     return pl.pallas_call(
         body,
         out_shape=out_shape,
+        cost_estimate=pl.CostEstimate(
+            flops=micros * 1000000000, bytes_accessed=micros * 1000000, transcendentals=0
+        ),
         compiler_params=pltpu.CompilerParams(vmem_limit_bytes=LIMIT),
         **more,
     )
@@ -233,6 +236,7 @@
         functools.partial(dispatch_kernel, capacity),
         (sds((slots, width + lanes), BF), sds((1, messages), I32)),
         name="dispatch",
+        micros=5,
     )(own_row, own_col, grad_out, rows4.astype(BF))
     arrived = across(
         payload.reshape(shards, capacity, width + lanes), split_axis=0, concat_axis=0
@@ -259,6 +263,7 @@
         ),
         scratch_shapes=[pltpu.VMEM((tokens, cols), F32)],
         name="scores",
+        micros=11,
     )(inputs, query_weight, sub_keys, picks, slot_col)
 
     back = local(
@@ -268,10 +273,12 @@
         in_specs=[
             pl.BlockSpec((128, width + lanes), lambda i: (i, 0)),
             pl.BlockSpec((table_rows, width), lambda i: (0, 0)),
+            pl.BlockSpec(memory_space=pl.ANY),
         ],
         out_specs=pl.BlockSpec((128, lanes), lambda i: (i, 0)),
         name="shard",
-    )(arrived, values)
+        micros=7,
+    )(arrived, values, weights)
     returned = across(back.reshape(shards, capacity, lanes), split_axis=0, concat_axis=0)
     returned = returned.reshape(slots, lanes)
 
@@ -290,6 +297,7 @@
         out_specs=pl.BlockSpec((table_rows, 512), lambda i: (0, i)),
         scratch_shapes=[pltpu.VMEM((table_rows, slots), BF)],
         name="table",
+        micros=9,
     )(arrived, arrived, arrived_weights)
     table_pieces = lax.all_to_all(
         table_part.reshape(groups, table_rows // groups, width), "rep", 0, 0, tiled=True
@@ -304,6 +312,7 @@
         (sds((shards, tokens, quarter), BF), sds((tokens, cols), BF)),
         scratch_shapes=[pltpu.VMEM((tokens, blocks * count // 128, 128), F32)],
         name="grads",
+        micros=7,
     )(returned, slot_col, weights, picks, sub_keys)
     input_grad = lax.dot_general(
         query_grad, query_weight, (((1,), (1,)), ((), ())), preferred_element_type=F32
@@ -331,7 +340,13 @@
         key_part.reshape(blocks, key_rows, half), "tab", 0, 0, axis_index_groups=members, tiled=True
     )
     key_part = jnp.transpose(key_part, (1, 0, 2)).reshape(key_rows, cols)
-    weight_grad, key_grad = lax.psum((weight_part, key_part), "rep")
+    share = jnp.concatenate([weight_part, key_part], axis=0).astype(BF)
+    share_rows = share.shape[0] // groups
+    pieces = lax.all_to_all(share.reshape(groups, share_rows, cols), "rep", 0, 0, tiled=True)
+    piece = jnp.sum(pieces.astype(F32), axis=0)
+    whole = lax.all_gather(piece, "rep", axis=0, tiled=True)
+    weight_grad = whole[:weight_rows]
+    key_grad = whole[weight_rows:]
     return (input_grad, weight_grad, key_grad, table_grad)
 
 

time: 305 us -> 291 us (0.954)
  blocking collectives: 116 us -> 90.7 us
  waiting for transfers between devices: 93.4 us -> 97.7 us
  starting transfers between devices: 12 us -> 15.6 us
  local copies, waits for them, and re-layouts: 12.4 us -> 15.8 us
    psum x1 -> x0, waiting for transfers between devices: 57.1 us -> none  [on_device(): weight_grad, key_grad = lax.psum((weight_part, key_part), 'rep')]
    all_to_all x1, waiting for transfers between devices: 0.01 us -> 52.5 us  [on_device(): across(payload.reshape(shards, capacity, width + lanes), split_axis=0, co...]
    all_to_all x1 -> x2, blocking collectives: 59.3 us -> 36.5 us  [the longest x1 20.4 us: on_device(): lax.all_to_all(share.reshape(groups, share_rows, cols), 'rep', 0, 0, tile...]
    all_gather x0 -> x1, waiting for transfers between devices: none -> 13.9 us  [on_device(): whole = lax.all_gather(piece, 'rep', axis=0, tiled=True)]
    all_to_all x1, waiting for transfers between devices: 12.4 us -> 7.41 us  [on_device(): across(half_grad, split_axis=0, concat_axis=0)]
    all_to_all x1, starting transfers between devices: 3.56 us -> 7.76 us  [on_device(): across(payload.reshape(shards, capacity, width + lanes), split_axis=0, co...]
    slice x0 -> x2, local copies, waits for them, and re-layouts: none -> 3.98 us  [the longest x1 2.31 us: on_device(): weight_grad = whole[:weight_rows]]
    unnamed x19 -> x15, local copies, waits for them, and re-layouts: 6.02 us -> 2.44 us
  transfers between devices with their start and end apart: 6 -> 6, of which waited for: 3 -> 4; matrix products, arithmetic and copies ran while one was open for 6% -> 8% of each run, Pallas kernels for 7% -> 7%
where the time goes in v2:
time: 291 us; the launch traced here: 289 us
  waiting for transfers between devices  97.7 us (34%)
  blocking collectives  90.7 us (31%)
  Pallas kernels  39 us (13%)
  local copies, waits for them, and re-layouts  15.8 us (5%)
  starting transfers between devices  15.6 us (5%)
  between operations  13.9 us (5%)
  matrix products  12.4 us (4%)
  other arithmetic  4.12 us (1%)
    all_to_all x1, waiting for transfers between devices, on_device(): across(payload.reshape(shards, capacity, width + lanes), split_axis=0, co...  52.5 us
    all_to_all x1, blocking collectives, on_device(): lax.all_to_all(table_part.reshape(groups, table_rows // groups, width), '...  36.8 us
    all_to_all x1, waiting for transfers between devices, on_device(): across(early, split_axis=0, concat_axis=0)  23.9 us
    all_to_all x1, blocking collectives, on_device(): lax.all_to_all(share.reshape(groups, share_rows, cols), 'rep', 0, 0, tile...  20.4 us
    all_to_all x1, blocking collectives, on_device(): across(back.reshape(shards, capacity, lanes), split_axis=0, concat_axis=0)  16.1 us
    all_gather x1, waiting for transfers between devices, on_device(): whole = lax.all_gather(piece, 'rep', axis=0, tiled=True)  13.9 us
    pallas_call x1, Pallas kernels, on_device(): local(functools.partial(score_kernel, heads), (sds((tokens, cols), BF), s...  11.1 us
    all_to_all x1, blocking collectives, on_device(): across(send_weights.reshape(shards, capacity, lanes), split_axis=0, conca...  10.2 us
  transfers between devices with their start and end apart: 6, of which 4 were waited for; matrix products, arithmetic and copies ran while one was open for 8% of the time, Pallas kernels for 7%

profile of v2, /device:TPU:1, one launch (start us, length us, event | category | flops | bytes accessed | tf_op | source)
XLA Modules:
  0.0 289.2 jit_solution(4189505901516949731)
XLA Ops:
  8.7 1.5 copy.18.own_col
  10.1 4.8 %dispatch.1 = (bf16[512,4224]{1,0:T(8,128)(2,1)}, s32[1,256]{1,0:T(1,128)}) custom-call(s32[1,256]{1,0:T(1,128)} %bitcast.70, s32[256,1]{1,0:T(8,128)} %copy.18.own_col, bf16[128,4096]{1,0:T(8,128)(2,1)} %grad.1, bf16[256,128]{1,0:T(8,128)(2,1)} %copy.19.rows), custom_call_target="tpu_custom_call" | custom-call | flops 5000000000 | bytes 5000000 | tf_op jit(solution)/shard_map/dispatch/pallas_call | solution.py:235
  15.0 7.8 %all-to-all-start = ((bf16[16,32,4224]{2,1,0:T(8,128)(2,1)}), bf16[16,32,4224]{2,1,0:T(8,128)(2,1)}, u32[]{:S(2)}, u32[]{:S(2)}) async-start(bf16[16,32,4224]{2,1,0:T(8,128)(2,1)} %bitcast.50), calls=%async_computation | async-start | bytes 8650752 | tf_op jit(solution)/shard_map/all_to_all | solution.py:241
  23.5 0.8 copy.21.slot_col
  24.3 11.1 %scores.1 = (bf16[128,1024]{1,0:T(8,128)(2,1)}, f32[128,128]{1,0:T(8,128)}, bf16[512,128]{1,0:T(8,128)(2,1)}) custom-call(bf16[128,4096]{1,0:T(8,128)(2,1)} %inputs.1, bf16[4096,1024]{1,0:T(8,128)(2,1)} %weight.1, bf16[1024,1024]{1,0:T(8,128)(2,1)} %keys.3, s32[128,128]{1,0:T(8,128)} %copy.20.picks, s32[256,1]{1,0:T(8,128)} %copy.21.slot_col), custom_call_target="tpu_custom_call" | custom-call | flops 11000000512 | bytes 11000000 | tf_op jit(solution)/shard_map/scores/pallas_call | solution.py:248
  35.5 52.5 %all-to-all-done = bf16[16,32,4224]{2,1,0:T(8,128)(2,1)} async-done(((bf16[16,32,4224]{2,1,0:T(8,128)(2,1)}), bf16[16,32,4224]{2,1,0:T(8,128)(2,1)}, u32[]{:S(2)}, u32[]{:S(2)}) %all-to-all-start) | async-done | bytes 4325408 | tf_op jit(solution)/shard_map/all_to_all | solution.py:241
  88.0 6.7 %shard.1 = f32[512,128]{1,0:T(8,128)} custom-call(bf16[512,4224]{1,0:T(8,128)(2,1)} %bitcast.8.arrived.rows, bf16[256,4096]{1,0:T(8,128)(2,1)} %values.1, f32[128,128]{1,0:T(8,128)} %get-tuple-element.13.after.soft), custom_call_target="tpu_custom_call" | custom-call | flops 7000000000 | bytes 7000000 | tf_op jit(solution)/shard_map/shard/pallas_call | solution.py:269
  94.7 16.1 %all_to_all.40 = f32[16,32,128]{2,1,0:T(8,128)} all-to-all(f32[16,32,128]{2,1,0:T(8,128)} %bitcast.65), channel_id=1, replica_groups=mesh['rep'=8,'tab'=16] {'tab'}, dimensions={0} | all-to-all | bytes 524288 | tf_op jit(solution)/shard_map/all_to_all | solution.py:282
  110.9 7.1 %grads.1 = (bf16[16,128,256]{2,1,0:T(8,128)(2,1)}, bf16[128,1024]{1,0:T(8,128)(2,1)}) custom-call(f32[512,128]{1,0:T(8,128)} %bitcast.64, s32[256,1]{1,0:T(8,128)} %copy.21.slot_col, f32[128,128]{1,0:T(8,128)} %get-tuple-element.13.after.soft, s32[128,128]{1,0:T(8,128)} %copy.20.picks, bf16[1024,1024]{1,0:T(8,128)(2,1)} %keys.3), custom_call_target="tpu_custom_call" | custom-call | flops 7000000000 | bytes 7000000 | tf_op jit(solution)/shard_map/grads/pallas_call | solution.py:310
  118.0 10.2 %all_to_all.41 = bf16[16,32,128]{2,1,0:T(8,128)(2,1)} all-to-all(bf16[16,32,128]{2,1,0:T(8,128)(2,1)S(1)} %bitcast.66), channel_id=1, replica_groups=mesh['rep'=8,'tab'=16] {'tab'}, dimensions={0} | all-to-all | bytes 262144 | tf_op jit(solution)/shard_map/all_to_all | solution.py:285
  128.2 9.2 %table.1 = bf16[256,4096]{1,0:T(8,128)(2,1)} custom-call(bf16[512,4224]{1,0:T(8,128)(2,1)} %bitcast.8.arrived.rows, bf16[512,4224]{1,0:T(8,128)(2,1)} %bitcast.8.arrived.rows, bf16[512,128]{1,0:T(8,128)(2,1)} %bitcast.67), custom_call_target="tpu_custom_call" | custom-call | flops 8999999488 | bytes 9000000 | tf_op jit(solution)/shard_map/table/pallas_call | solution.py:288
  137.4 36.8 %all_to_all.42 = bf16[8,32,4096]{2,1,0:T(8,128)(2,1)S(1)} all-to-all(bf16[8,32,4096]{2,1,0:T(8,128)(2,1)} %bitcast.57), channel_id=1, replica_groups=mesh['rep'=8,'tab'=16] {'rep'}, dimensions={0} | all-to-all | bytes 4194304 | tf_op jit(solution)/shard_map/all_to_all | solution.py:302
  174.2 3.8 %all-to-all-start.3 = ((bf16[16,128,256]{2,1,0:T(8,128)(2,1)}), bf16[16,128,256]{2,1,0:T(8,128)(2,1)S(1)}, u32[]{:S(2)}, u32[]{:S(2)}) async-start(bf16[16,128,256]{2,1,0:T(8,128)(2,1)} %get-tuple-element.16), calls=%async_computation.3 | async-start | bytes 2097152 | tf_op jit(solution)/shard_map/all_to_all | solution.py:333
  178.0 2.3 copy.33
  180.3 0.9 reshape.81
  181.2 1.0 copy.25
  182.2 1.1 reduce_sum.22
  183.4 1.1 copy-done
  184.5 1.5 pad_maximum_fusion
  186.0 7.4 %all-to-all-done.3 = bf16[16,128,256]{2,1,0:T(8,128)(2,1)S(1)} async-done(((bf16[16,128,256]{2,1,0:T(8,128)(2,1)}), bf16[16,128,256]{2,1,0:T(8,128)(2,1)S(1)}, u32[]{:S(2)}, u32[]{:S(2)}) %all-to-all-start.3) | async-done | bytes 1048608 | tf_op jit(solution)/shard_map/all_to_all | solution.py:333
  193.4 3.9 %all-to-all-start.2 = ((bf16[16,128,512]{2,1,0:T(8,128)(2,1)}), bf16[16,128,512]{2,1,0:T(8,128)(2,1)S(1)}, u32[]{:S(2)}, u32[]{:S(2)}) async-start(bf16[16,128,512]{2,1,0:T(8,128)(2,1)} %pad_maximum_fusion), calls=%async_computation.2 | async-start | bytes 4194304 | tf_op jit(solution)/shard_map/all_to_all | solution.py:330
  197.4 1.4 copy.26
  198.8 23.9 %all-to-all-done.2 = bf16[16,128,512]{2,1,0:T(8,128)(2,1)S(1)} async-done(((bf16[16,128,512]{2,1,0:T(8,128)(2,1)}), bf16[16,128,512]{2,1,0:T(8,128)(2,1)S(1)}, u32[]{:S(2)}, u32[]{:S(2)}) %all-to-all-start.2) | async-done | bytes 2097184 | tf_op jit(solution)/shard_map/all_to_all | solution.py:330
  222.6 1.7 fusion
  224.3 7.2 %all_to_all.43 = bf16[4,64,256]{2,1,0:T(8,128)(2,1)S(1)} all-to-all(bf16[4,64,256]{2,1,0:T(8,128)(2,1)S(1)} %fusion), channel_id=1, replica_groups={{0,1,2,3},{4,5,6,7},{8,9,10,11},{12,13,14,15},{16,17,18,19},{20,21,22,2..., dimensions={0} | all-to-all | bytes 262144 | tf_op jit(solution)/shard_map/all_to_all | solution.py:339
  231.6 3.5 %convolution_convert_fusion.1 = bf16[256,1024]{1,0:T(8,128)(2,1)S(1)} fusion(bf16[2048,1024]{1,0:T(8,128)(2,1)} %all-gather.4.cloned.1.call-done, bf16[2048,512]{1,0:T(8,128)(2,1)S(1)} %bitcast.56), kind=kOutput, calls=%fused_computation.3 | convolution fusion | flops 1074003968 | bytes 5767168 | tf_op jit(solution)/shard_map/dot_general | solution.py:24
  235.1 20.4 %all_to_all.44 = bf16[8,40,1024]{2,1,0:T(8,128)(2,1)S(1)} all-to-all(bf16[8,40,1024]{2,1,0:T(8,128)(2,1)S(1)} %bitcast.54), channel_id=1, replica_groups=mesh['rep'=8,'tab'=16] {'rep'}, dimensions={0} | all-to-all | bytes 1310720 | tf_op jit(solution)/shard_map/all_to_all | solution.py:345
  256.3 7.2 %convolution_convert_fusion = bf16[128,4096]{1,0:T(8,128)(2,1)} fusion(bf16[128,1024]{1,0:T(8,128)(2,1)S(1)} %copy-done.2, bf16[4096,1024]{1,0:T(8,128)(2,1)} %weight.1), kind=kOutput, calls=%fused_computation | convolution fusion | flops 1074266112 | bytes 9699328 | tf_op jit(solution)/shard_map/dot_general | solution.py:317
  263.5 13.9 %all-gather.6.cloned.1.call-done = f32[320,1024]{1,0:T(8,128)} async-done(((f32[40,1024]{1,0:T(8,128)}), f32[320,1024]{1,0:T(8,128)}) %all-gather.6.cloned.1.call-update) | async-done | bytes 1310736 | tf_op jit(solution)/shard_map/all_gather | solution.py:347
  277.4 1.7 slice.19
  279.1 2.3 slice.18
  281.4 1.3 copy.35
  (29 shorter events, 3.4 us)
Async XLA Ops:
  15.0 7.8 %copy-start.5 = (s32[128,2,2,32]{0,3,2,1:T(8,128)S(1)}, s32[128,2,2,32]{0,3,2,1:T(8,128)}, u32[]{:S(2)}) copy-start(s32[128,2,2,32]{0,3,2,1:T(8,128)} %param.15) | copy-start | bytes 196612
  15.0 8.5 %copy-start.6 = (s32[1,256]{1,0:T(1,128)S(1)}, s32[1,256]{1,0:T(1,128)}, u32[]{:S(2)}) copy-start(s32[1,256]{1,0:T(1,128)} %get-tuple-element.12) | copy-start | bytes 3076
  15.0 73.0 %all-to-all-start = ((bf16[16,32,4224]{2,1,0:T(8,128)(2,1)}), bf16[16,32,4224]{2,1,0:T(8,128)(2,1)}, u32[]{:S(2)}, u32[]{:S(2)}) async-start(bf16[16,32,4224]{2,1,0:T(8,128)(2,1)} %bitcast.50), calls=%async_computation | async-start | bytes 8650752 | tf_op jit(solution)/shard_map/all_to_all | solution.py:241
  22.7 208.8 %all-gather.4.cloned.1.call-start = ((), (), s32[]{:S(2)}) async-start(), calls=%async_computation.8 | async-start | bytes 4456448 | tf_op jit(solution)/shard_map/all_gather | solution.py:334
  110.9 7.1 %copy-start.4 = (bf16[512,128]{1,0:T(8,128)(2,1)S(1)}, bf16[512,128]{1,0:T(8,128)(2,1)}, u32[]{:S(2)}) copy-start(bf16[512,128]{1,0:T(8,128)(2,1)} %get-tuple-element.17) | copy-start | bytes 393220
  174.2 6.2 %copy-start.3 = (bf16[128,1024]{1,0:T(8,128)(2,1)S(1)}, bf16[128,1024]{1,0:T(8,128)(2,1)}, u32[]{:S(2)}) copy-start(bf16[128,1024]{1,0:T(8,128)(2,1)} %get-tuple-element.15) | copy-start | bytes 786436
  174.2 19.2 %all-to-all-start.3 = ((bf16[16,128,256]{2,1,0:T(8,128)(2,1)}), bf16[16,128,256]{2,1,0:T(8,128)(2,1)S(1)}, u32[]{:S(2)}, u32[]{:S(2)}) async-start(bf16[16,128,256]{2,1,0:T(8,128)(2,1)} %get-tuple-element.16), calls=%async_computation.3 | async-start | bytes 2097152 | tf_op jit(solution)/shard_map/all_to_all | solution.py:333
  178.0 85.5 %all-gather.8.cloned.1.call-start = ((), (), s32[]{:S(2)}) async-start(), calls=%async_computation.10 | async-start | bytes 2359296 | tf_op jit(solution)/shard_map/all_gather | solution.py:306
  183.3 1.2 copy-start
  193.4 29.2 %all-to-all-start.2 = ((bf16[16,128,512]{2,1,0:T(8,128)(2,1)}), bf16[16,128,512]{2,1,0:T(8,128)(2,1)S(1)}, u32[]{:S(2)}, u32[]{:S(2)}) async-start(bf16[16,128,512]{2,1,0:T(8,128)(2,1)} %pad_maximum_fusion), calls=%async_computation.2 | async-start | bytes 4194304 | tf_op jit(solution)/shard_map/all_to_all | solution.py:330
  197.3 80.1 %all-gather.6.cloned.1.call-start = ((), (), s32[]{:S(2)}) async-start(), calls=%async_computation.9 | async-start | bytes 1474560 | tf_op jit(solution)/shard_map/all_gather | solution.py:347
  235.0 21.2 %copy-start.2 = (bf16[128,1024]{1,0:T(8,128)(2,1)S(1)}, bf16[128,1024]{1,0:T(8,128)(2,1)}, u32[]{:S(2)}) copy-start(bf16[128,1024]{1,0:T(8,128)(2,1)} %get-tuple-element.14) | copy-start | bytes 786436
  263.5 17.9 %copy-start.1 = (bf16[256,4096]{1,0:T(8,128)(2,1)S(1)}, bf16[256,4096]{1,0:T(8,128)(2,1)}, u32[]{:S(2)}) copy-start(bf16[256,4096]{1,0:T(8,128)(2,1)} %all-gather.8.cloned.1.call-done) | copy-start | bytes 6291460
Sparse Core Ops, SparseCore 0:
  118.1 53.5 all-gather.3
  183.4 25.7 all-gather.7
  256.4 20.9 all-gather.5

commit v3 on v0

v3 whole, which is shorter than its diff:
```python
import jax
import jax.numpy as jnp
from jax import lax
from jax.experimental import pallas as pl
from jax.experimental.pallas import tpu as pltpu
from jax.sharding import PartitionSpec as P

BF = jnp.bfloat16
F32 = jnp.float32
I32 = jnp.int32


def dot_nn(a, b):
    return lax.dot_general(a, b, (((1,), (0,)), ((), ())), preferred_element_type=F32)


def dot_nt(a, b):
    return lax.dot_general(a, b, (((1,), (1,)), ((), ())), preferred_element_type=F32)


def dot_tn(a, b):
    return lax.dot_general(a, b, (((0,), (0,)), ((), ())), preferred_element_type=F32)


def three(x):
    a = x.astype(BF)
    rest = x - a.astype(F32)
    b = rest.astype(BF)
    c = (rest - b.astype(F32)).astype(BF)
    return a, b, c


def iota(shape, dim):
    return lax.broadcasted_iota(I32, shape, dim)

MESH = pl.DeviceIdType.MESH
TURNS = (0, 1, 3, 2)


def whole_kernel(
    own, rows_t, picks_t, grad, inputs, weight, keys, values,
    in_grad, w_grad, k_grad, t_grad,
    pay, arr, inp, wt, key, val, acc, low, soft, score, wsend, wrecv, back, ret, spread,
    tpart, tcore, thalf, tz, placed, hsend, hrecv, lrecv, qg, gq, ginp, ksend, krecv, wacc,
    psend, precv, load_sem, ssem, rsem,
):
    heads, tokens = own.shape
    width = grad.shape[1]
    shards, capacity, wide = pay.shape
    lanes = picks_t.shape[0]
    blocks = 2 * heads
    top = lanes // blocks
    cols = acc.shape[1]
    half = cols // blocks
    count = key.shape[0]
    tiles = count // 128
    table_rows = val.shape[0]
    slots = shards * capacity
    side = 4
    band = slots // side
    me, r = lax.axis_index("tab"), lax.axis_index("rep")
    mx, my = me // side, lax.rem(me, side)
    mz, mc = r // 2, lax.rem(r, 2)
    used = [0]

    def at_tab(dx, dy):
        return lax.rem(mx + dx, side) * side + lax.rem(my + dy, side)

    def send(src, dst, device, numbers=None):
        if numbers is None:
            numbers = (used[0], used[0])
            used[0] += 1
        copy = pltpu.make_async_remote_copy(
            src_ref=src,
            dst_ref=dst,
            send_sem=ssem.at[numbers[0]],
            recv_sem=rsem.at[numbers[1]],
            device_id=device,
            device_id_type=MESH,
        )
        copy.start()
        return copy

    loads = [pltpu.make_async_copy(inputs, inp, load_sem.at[0])]
    depth = width // 4
    for i in range(4):
        piece = pl.ds(i * depth, depth)
        loads.append(pltpu.make_async_copy(weight.at[piece], wt.at[piece], load_sem.at[1 + i]))
    loads.append(pltpu.make_async_copy(keys, key, load_sem.at[5]))
    loads.append(pltpu.make_async_copy(values, val, load_sem.at[6]))
    for load in loads:
        load.start()
    barrier = pltpu.get_barrier_semaphore()
    for d in range(1, shards):
        pl.semaphore_signal(
            barrier, inc=1, device_id={"tab": lax.rem(me + d, shards)}, device_id_type=MESH
        )
    for d in range(1, 8):
        pl.semaphore_signal(
            barrier, inc=1, device_id={"rep": lax.rem(r + d, 8)}, device_id_type=MESH
        )

    owned = jnp.concatenate([own[h : h + 1, :] for h in range(heads)], axis=1)
    messages = heads * tokens
    across = jnp.broadcast_to(owned, (messages, messages))
    same = across == across.T
    earlier = iota((messages, messages), 0) < iota((messages, messages), 1)
    rank = jnp.sum(jnp.where(same & earlier, 1.0, 0.0), axis=0, keepdims=True).astype(I32)
    place = owned * capacity + rank
    row_lanes = []
    for h in range(heads):
        one = rows_t[h * top : (h + 1) * top, :].astype(F32)
        row_lanes.append(jnp.concatenate([one] * blocks, axis=0).T)
    row_lanes = jnp.concatenate(row_lanes, axis=0).astype(BF)

    outgoing = []
    for turn, dx in enumerate(TURNS):
        gx = lax.rem(mx + dx, side)
        hit = jnp.where(iota((band, messages), 0) + gx * band == place, 1.0, 0.0)
        either = hit[:, :tokens]
        for h in range(1, heads):
            either = either + hit[:, h * tokens : (h + 1) * tokens]
        either = either.astype(BF)
        here = pl.ds(gx * side, side)
        for at in range(0, width, 512):
            block = dot_nn(either, grad[:, at : at + 512]).astype(BF)
            pay[here, :, at : at + 512] = block.reshape(side, capacity, 512)
        block = dot_nn(hit.astype(BF), row_lanes).astype(BF)
        pay[here, :, width:] = block.reshape(side, capacity, wide - width)
        if turn == 0:
            pl.semaphore_wait(barrier, shards + 6)
        for dy in TURNS:
            if dx or dy:
                p = at_tab(dx, dy)
                outgoing.append(send(pay.at[p], arr.at[me], {"tab": p}))
            else:
                outgoing.append(None)
    arr[me] = pay[me]

    loads[0].wait()
    for i in range(4):
        loads[1 + i].wait()
        part = dot_nn(inp[:, i * depth : (i + 1) * depth], wt[i * depth : (i + 1) * depth, :])
        acc[...] = part if i == 0 else acc[...] + part
    low[...] = acc[...].astype(BF)
    lows = []
    for d in range(1, 8):
        p = lax.rem(r + d, 8)
        piece = pl.ds(pl.multiple_of((p // 2) * half, half), half)
        lows.append(send(low.at[:, piece], lrecv.at[r], {"rep": p}))
    lrecv[r] = low[:, pl.ds(pl.multiple_of(mz * half, half), half)]
    pick = picks_t[...].T
    low_pick = pick % 128
    high_pick = pick // 128
    lane_block = iota((tokens, lanes), 1) // top
    head_of = lane_block // 2
    chosen = jnp.zeros((tokens, lanes), F32)
    loads[5].wait()
    for b in range(blocks):
        parts = three(acc[:, b * half : (b + 1) * half])
        for j in range(tiles):
            names = key[j * 128 : (j + 1) * 128, b * half : (b + 1) * half]
            part = dot_nt(parts[2], names) + dot_nt(parts[1], names) + dot_nt(parts[0], names)
            got = jnp.take_along_axis(part, low_pick, axis=1)
            chosen = jnp.where((high_pick == j) & (lane_block == b), got, chosen)
    even = lane_block % 2 == 0
    other = jnp.where(
        even, pltpu.roll(chosen, lanes - top, axis=1), pltpu.roll(chosen, top, axis=1)
    )
    scores = chosen + other

    def over_heads(x, fill, reduce):
        out = jnp.zeros((tokens, lanes), F32)
        for h in range(heads):
            one = reduce(jnp.where(head_of == h, x, fill), axis=1, keepdims=True)
            out = jnp.where(head_of == h, one, out)
        return out

    raised = jnp.exp(scores - over_heads(scores, -jnp.inf, jnp.max))
    weights = raised / (over_heads(raised, 0.0, jnp.sum) * 0.5)
    soft[...] = weights
    low_soft = weights.astype(BF).astype(F32)

    def hits(h):
        column = jnp.broadcast_to(place[:, h * tokens : (h + 1) * tokens], (tokens, tokens)).T
        column = jnp.concatenate([column] * (slots // tokens), axis=1)
        return jnp.where(iota((tokens, slots), 1) == column, 1.0, 0.0).astype(BF)

    sent = jnp.zeros((slots, lanes), F32)
    for h in range(heads):
        turned = low_soft if h == 0 else pltpu.roll(low_soft, lanes - h * 2 * top, axis=1)
        sent = sent + dot_tn(hits(h), turned.astype(BF))
    wsend[...] = sent.astype(BF).reshape(shards, capacity, lanes)
    weighing = []
    for dx in TURNS:
        for dy in TURNS:
            if dx or dy:
                p = at_tab(dx, dy)
                weighing.append(send(wsend.at[p], wrecv.at[me], {"tab": p}))
    wrecv[me] = wsend[me]

    loads[6].wait()
    returning = []
    for turn, dx in enumerate(TURNS):
        for copy in outgoing[turn * side : (turn + 1) * side]:
            if copy is not None:
                copy.wait_recv()
        gx = lax.rem(mx - dx + side, side)
        here = pl.ds(gx * side, side)
        product = dot_nt(arr[here, :, :width].reshape(band, width), val[...])
        name = arr[here, :, width:].reshape(band, lanes).astype(I32)
        out = jnp.zeros((band, lanes), F32)
        for j in range(table_rows // 128):
            got = jnp.take_along_axis(product[:, j * 128 : (j + 1) * 128], name % 128, axis=1)
            out = jnp.where(name // 128 == j, got, out)
        back[here] = out.reshape(side, capacity, lanes)
        for dy in TURNS:
            if dx or dy:
                p = at_tab(side - dx, side - dy)
                returning.append(send(back.at[p], ret.at[me], {"tab": p}))
    ret[me] = back[me]
    spreading = []
    piece_width = width // shards
    for dx in TURNS:
        for dy in TURNS:
            if dx or dy:
                p = at_tab(dx, dy)
                piece = pl.ds(pl.multiple_of(p * piece_width, piece_width), piece_width)
                spreading.append(send(inp.at[:, piece], ginp.at[me], {"tab": p}))
    ginp[me] = inp[:, pl.ds(pl.multiple_of(me * piece_width, piece_width), piece_width)]

    for copy in weighing:
        copy.wait_recv()

    def spread_band(g, carry):
        here = pl.ds(g * side, side)
        row_t = arr[here, :, width:].reshape(band, lanes).astype(F32).T
        soft_t = wrecv[here].reshape(band, lanes).astype(F32).T
        names = iota((table_rows, band), 0).astype(F32)
        held = jnp.zeros((table_rows, band), F32)
        for k in range(top):
            held = held + jnp.where(names == row_t[k : k + 1], soft_t[k : k + 1], 0.0)
        spread[:, pl.ds(pl.multiple_of(g * band, band), band)] = held.astype(BF)
        return carry

    lax.fori_loop(0, side, spread_band, 0)

    for copy in returning:
        copy.wait_recv()
    parts = three(ret[...].reshape(slots, lanes))
    slot_grad = jnp.zeros((tokens, lanes), F32)
    for h in range(heads):
        hit = hits(h)
        got = dot_nn(hit, parts[2]) + dot_nn(hit, parts[1]) + dot_nn(hit, parts[0])
        slot_grad = jnp.where(head_of == h, got, slot_grad)
    weights = soft[...]
    mean = over_heads(weights * slot_grad, 0.0, jnp.sum) * 0.5
    score[0] = weights * (slot_grad - mean)
    score[1] = low_pick.astype(F32)
    score[2] = (high_pick + tiles * lane_block).astype(F32)

    def place_band(i, carry):
        here = pl.ds(pl.multiple_of(i * 8, 8), 8)
        amount, low8, high8 = score[0, here, :], score[1, here, :], score[2, here, :]
        high_names = iota((blocks * tiles, lanes), 0).astype(F32)
        low_names = iota((128, lanes), 0).astype(F32)
        for u in range(8):
            left = jnp.where(high_names == high8[u : u + 1], amount[u : u + 1], 0.0).astype(BF)
            right = jnp.where(low_names == low8[u : u + 1], 1.0, 0.0).astype(BF)
            placed[i * 8 + u] = dot_nt(left, right)
        return carry

    lax.fori_loop(0, tokens // 8, place_band, 0)
    for b in range(blocks):
        total = jnp.zeros((tokens, half), F32)
        for j in range(tiles):
            sums = placed[:, b * tiles + j, :].astype(BF)
            hsend[2 * b + j % 2, :, (j // 2) * 128 : (j // 2 + 1) * 128] = sums
            total = total + dot_nn(sums, key[j * 128 : (j + 1) * 128, b * half : (b + 1) * half])
        qg[:, b * half : (b + 1) * half] = total.astype(BF)

    middle = cols // 2
    left, right = pl.ds(0, middle), pl.ds(middle, middle)
    first = []
    for d in (1, 3, 2):
        p = at_tab(0, d)
        first.append((d, 0, send(qg.at[:, left], gq.at[me, :, left], {"tab": p})))
        p = at_tab(d, 0)
        first.append((d, 1, send(qg.at[:, right], gq.at[me, :, right], {"tab": p})))
    second = []

    def forward(e, kind):
        for d in (1, 3, 2):
            if kind == 0:
                part = gq.at[at_tab(0, side - e), :, left]
                second.append(send(part, part, {"tab": at_tab(d, 0)}))
            else:
                part = gq.at[at_tab(side - e, 0), :, right]
                second.append(send(part, part, {"tab": at_tab(0, d)}))

    gq[me] = qg[...]
    for kind in (0, 1):
        forward(0, kind)
    halves = []
    for d in range(1, 8):
        p = lax.rem(r + d, 8)
        halves.append(send(hsend.at[p], hrecv.at[r], {"rep": p}))
    hrecv[r] = hsend[r]

    for at in range(0, width, 512):
        column = arr[:, :, at : at + 512].reshape(slots, 512)
        tpart[:, at : at + 512] = dot_nn(spread[...], column).astype(BF)
    own_half = table_rows // 2
    mate = mz * 2 + 1 - mc
    mine = pl.ds(pl.multiple_of(mc * own_half, own_half), own_half)
    theirs = pl.ds(pl.multiple_of((1 - mc) * own_half, own_half), own_half)
    swap = send(tpart.at[theirs], tcore, {"rep": mate})
    for e, kind, copy in first:
        copy.wait_recv()
        forward(e, kind)
    for at in range(0, width, 512):
        in_grad[:, at : at + 512] = dot_nt(qg[...], wt[at : at + 512, :]).astype(BF)

    swap.wait_recv()
    quarter = own_half // 4
    for z in range(4):
        row = pl.multiple_of(mc * own_half, own_half) + z * quarter
        mixed = tpart[pl.ds(row, quarter), :].astype(F32)
        mixed = mixed + tcore[z * quarter : (z + 1) * quarter, :].astype(F32)
        thalf[z] = mixed.astype(BF)
    table_in = []
    for d in (1, 3, 2):
        z = lax.rem(mz + d, 4)
        table_in.append(send(thalf.at[z], tz.at[mz], {"rep": z * 2 + mc}))
    tz[mz] = thalf[mz]

    for copy in lows + halves:
        copy.wait_recv()
    key_part = dot_tn(
        hrecv[...].reshape(8 * tokens, count // 2), lrecv[...].reshape(8 * tokens, half)
    )
    key_rows = count // shards
    ksend[...] = key_part.astype(BF).reshape(8, key_rows, half)
    key_base = used[0]
    used[0] += shards
    key_out = []
    for i in range(2):
        for dx in range(side):
            x = lax.rem(mx + dx, side)
            p = x * side + 2 * mc + i
            copy = pltpu.make_async_remote_copy(
                src_ref=ksend.at[x * 2 + i],
                dst_ref=krecv.at[me],
                send_sem=ssem.at[key_base + i * side + dx],
                recv_sem=rsem.at[key_base + me],
                device_id={"tab": p},
                device_id_type=MESH,
            )
            key_out.append((i, dx, copy))
            if dx:
                copy.start()
            else:

                @pl.when(my != 2 * mc + i)
                def _(copy=copy):
                    copy.start()

                @pl.when(my == 2 * mc + i)
                def _(x=x, i=i):
                    krecv[me] = ksend[x * 2 + i]

    for copy in table_in:
        copy.wait_recv()
    summed = tz[0].astype(F32)
    for z in range(1, 4):
        summed = summed + tz[z].astype(F32)
    table_row = pl.multiple_of(mc * own_half + mz * quarter, quarter)
    table_mine = t_grad.at[pl.ds(table_row, quarter)]
    table_mine[...] = summed.astype(BF)
    table_out = []
    for d in (1, 3, 2):
        z = lax.rem(mz + d, 4)
        table_out.append((d, send(table_mine, table_mine, {"rep": z * 2 + mc})))
    table_last = [send(table_mine, table_mine, {"rep": mate})]

    key_last = used[0]
    used[0] += 8
    keeper = my // 2
    key_block = pl.ds(pl.multiple_of(mz * half, half), half)

    def key_share(d):
        return pltpu.make_async_remote_copy(
            src_ref=k_grad.at[:, key_block],
            dst_ref=k_grad.at[:, key_block],
            send_sem=ssem.at[key_last + d],
            recv_sem=rsem.at[key_last + mz],
            device_id={"rep": lax.rem(r + d, 8)},
            device_id_type=MESH,
        )

    @pl.when(keeper == mc)
    def _():
        for d in range(1, shards):
            q = lax.rem(me + d, shards)
            pltpu.make_async_remote_copy(
                src_ref=ksend.at[0],
                dst_ref=krecv.at[q],
                send_sem=ssem.at[key_base],
                recv_sem=rsem.at[key_base + q],
                device_id={"tab": q},
                device_id_type=MESH,
            ).wait_recv()
        total = krecv[0].astype(F32)
        for q in range(1, shards):
            total = total + krecv[q].astype(F32)
        k_grad[:, key_block] = total
        for d in range(1, 8):
            key_share(d).start()

    for copy in spreading + second:
        copy.wait_recv()
    for g in range(side):
        near = ginp[g * side : (g + 1) * side].reshape(side * tokens, piece_width)
        far = gq[g * side : (g + 1) * side].reshape(side * tokens, cols)
        part = dot_tn(near, far)
        wacc[...] = part if g == 0 else wacc[...] + part
    share = piece_width // 8
    psend[...] = wacc[...].astype(BF).reshape(8, share, cols)
    sums_in = []
    for d in range(1, 8):
        p = lax.rem(r + d, 8)
        sums_in.append(send(psend.at[p], precv.at[r], {"rep": p}))
    precv[r] = psend[r]
    for d, copy in table_out:
        copy.wait_recv()
        row = pl.multiple_of(mc * own_half + lax.rem(mz - d + 4, 4) * quarter, quarter)
        part = t_grad.at[pl.ds(row, quarter)]
        table_last.append(send(part, part, {"rep": mate}))
    for copy in sums_in:
        copy.wait_recv()
    total = precv[0].astype(F32)
    for q in range(1, 8):
        total = total + precv[q].astype(F32)
    mine = w_grad.at[pl.ds(pl.multiple_of(r * share, share), share)]
    mine[...] = total
    sums_out, sums_last = [], []
    for d in (1, 3, 2):
        z = lax.rem(mz + d, 4)
        sums_out.append((d, send(mine, mine, {"rep": z * 2 + mc})))
    sums_last.append(send(mine, mine, {"rep": mate}))
    for d, copy in sums_out:
        copy.wait_recv()
        row = pl.multiple_of((lax.rem(mz - d + 4, 4) * 2 + mc) * share, share)
        part = w_grad.at[pl.ds(row, share)]
        sums_last.append(send(part, part, {"rep": mate}))

    for b in range(4):

        @pl.when((b != mz) | (keeper != mc))
        def _(b=b):
            part = k_grad.at[:, b * half : (b + 1) * half]
            pltpu.make_async_remote_copy(
                src_ref=part,
                dst_ref=part,
                send_sem=ssem.at[key_last],
                recv_sem=rsem.at[key_last + b],
                device_id={"rep": mate},
                device_id_type=MESH,
            ).wait_recv()

    for copy in table_last + sums_last:
        copy.wait_recv()
    for i, dx, copy in key_out:
        if dx:
            copy.wait_send()
        else:

            @pl.when(my != 2 * mc + i)
            def _(copy=copy):
                copy.wait_send()

    @pl.when(keeper == mc)
    def _():
        for d in range(1, 8):
            key_share(d).wait_send()

    done = [copy for copy in outgoing if copy is not None] + lows + weighing + returning
    done = done + spreading + [copy for _, _, copy in first] + second + halves + [swap]
    done = done + table_in + [copy for _, copy in table_out] + table_last
    done = done + sums_in + [copy for _, copy in sums_out] + sums_last
    for copy in done:
        copy.wait_send()
    assert used[0] <= ssem.shape[0]


def sds(shape, dtype):
    return jax.ShapeDtypeStruct(shape, dtype)


def on_device(inputs, grad_out, query_weight, sub_keys, values, owner, slot_rows, sub_index):
    tokens, width = inputs.shape
    cols = query_weight.shape[1]
    count = sub_keys.shape[0]
    heads, top = slot_rows.shape[1:]
    blocks = 2 * heads
    lanes = blocks * top
    half = cols // blocks
    shards = lax.axis_size("tab")
    capacity = 2 * tokens * heads // shards
    slots = shards * capacity
    table_rows = values.shape[0]
    own = jnp.transpose(owner, (1, 2, 0)).reshape(heads, tokens)
    rows_t = jnp.transpose(slot_rows, (1, 2, 0)).reshape(heads * top, tokens)
    picks_t = jnp.transpose(sub_index, (1, 2, 3, 0)).reshape(lanes, tokens)
    vmem = pl.BlockSpec(memory_space=pltpu.VMEM)
    anywhere = pl.BlockSpec(memory_space=pl.ANY)
    V = pltpu.VMEM
    wide = width + lanes
    return pl.pallas_call(
        whole_kernel,
        out_shape=(
            sds((tokens, width), BF),
            sds((width // shards, cols), F32),
            sds((count // shards, cols), F32),
            sds((table_rows, width), BF),
        ),
        in_specs=[vmem] * 4 + [anywhere] * 4,
        out_specs=(vmem,) * 4,
        scratch_shapes=[
            V((shards, capacity, wide), BF),
            V((shards, capacity, wide), BF),
            V((tokens, width), BF),
            V((width, cols), BF),
            V((count, cols), BF),
            V((table_rows, width), BF),
            V((tokens, cols), F32),
            V((tokens, cols), BF),
            V((tokens, lanes), F32),
            V((3, tokens, lanes), F32),
            V((shards, capacity, lanes), BF),
            V((shards, capacity, lanes), BF),
            V((shards, capacity, lanes), F32),
            V((shards, capacity, lanes), F32),
            V((table_rows, slots), BF),
            V((table_rows, width), BF),
            V((table_rows // 2, width), BF),
            V((4, table_rows // 8, width), BF),
            V((4, table_rows // 8, width), BF),
            V((tokens, blocks * count // 128, 128), F32),
            V((8, tokens, count // 2), BF),
            V((8, tokens, count // 2), BF),
            V((8, tokens, half), BF),
            V((tokens, cols), BF),
            V((shards, tokens, cols), BF),
            V((shards, tokens, width // shards), BF),
            V((8, count // shards, half), BF),
            V((shards, count // shards, half), BF),
            V((width // shards, cols), F32),
            V((8, width // shards // 8, cols), BF),
            V((8, width // shards // 8, cols), BF),
            pltpu.SemaphoreType.DMA((7,)),
            pltpu.SemaphoreType.DMA((192,)),
            pltpu.SemaphoreType.DMA((192,)),
        ],
        compiler_params=pltpu.CompilerParams(
            collective_id=0, has_side_effects=True, vmem_limit_bytes=60 * 1024 * 1024
        ),
        name="whole",
    )(own, rows_t, picks_t, grad_out, inputs, query_weight, sub_keys, values)


def solution(mesh):
    placed = (
        P(("rep", "tab"), None),
        P(("rep", "tab"), None),
        P(),
        P(),
        P("tab", None),
        P(("rep", "tab"), None, None),
        P(("rep", "tab"), None, None),
        P(("rep", "tab"), None, None, None),
    )
    return jax.shard_map(
        on_device,
        mesh=mesh,
        in_specs=placed,
        out_specs=(P(("rep", "tab"), None), P("tab", None), P("tab", None), P("tab", None)),
        check_vma=False,
    )
```

time: 428 us -> 156 us (0.36)
  waiting for transfers between devices: 184 us -> 0 us
  Pallas kernels: 0 us -> 150 us
  blocking collectives: 62.4 us -> 0 us
  other arithmetic: 54.8 us -> 0 us
  local copies, waits for them, and re-layouts: 46.2 us -> 5.44 us
  matrix products: 39 us -> 0 us
  starting transfers between devices: 24.4 us -> 0 us
  between operations: 14.3 us -> 0.67 us
    pallas_call x0 -> x1, Pallas kernels: none -> 150 us  [on_device(): pl.pallas_call(whole_kernel, out_shape=(sds((tokens, width), BF), sds((wi...]
    reduce_scatter x1 -> x0, waiting for transfers between devices: 129 us -> none  [on_device(): lax.psum_scatter(grad_term(input_blocks, grad_blocks, query_grad, query_b...]
    psum x1 -> x0, blocking collectives: 62.4 us -> none  [on_device(): local_sum, table_sum = lax.psum((local, table_part), 'rep')]
    all_to_all x4 -> x0, waiting for transfers between devices: 54.6 us -> none  [the longest x1 46.5 us: on_device(): lax.all_to_all(payload.reshape(shards, capacity, model_width), 'tab', spl...]
    reduce_sum x6 -> x0, other arithmetic: 38.6 us -> none  [the longest x2 16.5 us: place_block(): return jnp.sum(jnp.where(equal, block_spread[:, :, :, None], 0.0), axis=2)]
    dot_general x12 -> x0, matrix products: 37.4 us -> none  [the longest x1 7.43 us: on_device(): lax.dot_general(query_grad, query_weight, (((1,), (1,)), ((), ())), prefe...]
    all_to_all x4 -> x0, starting transfers between devices: 24.1 us -> none  [the longest x1 7.58 us: on_device(): lax.all_to_all(send_weights.reshape(shards, capacity, top_count), 'tab',...]
    concatenate x1 -> x0, other arithmetic: 9.21 us -> none  [grad_term(): joined = jnp.concatenate([weight_part, key_part], axis=1)]
  transfers between devices with their start and end apart: 6 -> 0, of which waited for: 4 -> 0; matrix products, arithmetic and copies ran while one was open for 8% -> 0% of each run, Pallas kernels for 0% -> 0%
where the time goes in v3:
time: 156 us
  Pallas kernels  150 us (96%)
  local copies, waits for them, and re-layouts  5.44 us (3%)
    pallas_call x1, Pallas kernels, on_device(): pl.pallas_call(whole_kernel, out_shape=(sds((tokens, width), BF), sds((wi...  150 us
    unnamed x10, local copies, waits for them, and re-layouts  5.44 us

profile of v3, /device:TPU:1, one launch (start us, length us, event | category | flops | bytes accessed | tf_op | source)
XLA Modules:
  0.0 155.7 jit_solution(14660855600356725574)
XLA Ops:
  0.6 149.6 %whole.1 = (bf16[128,4096]{1,0:T(8,128)(2,1)}, f32[256,1024]{1,0:T(8,128)}, f32[64,1024]{1,0:T(8,128)}, bf16[256,4096]{1,0:T(8,128)(2,1)}) custom-call(s32[2,128]{1,0:T(2,128)} %bitcast.13, s32[64,128]{1,0:T(8,128)} %bitcast.12, s32[128,128]{1,0:T(8,128)} %bitcast.11, bf16[128,4096]{1,0:T(8,128)(2,1)} %grad.1, bf16[128,4096]{1,0:T(8,128)(2,1)} %inputs.1, ...), custom_call_target="tpu_custom_call" | custom-call | tf_op jit(solution)/shard_map/whole/pallas_call | solution.py:519
  150.2 0.0 copy-start.1
  150.3 0.0 copy-start.2
  150.3 0.0 copy-start
  150.3 2.4 %copy.17 = bf16[128,4096]{1,0:T(8,128)(2,1)} copy(bf16[128,4096]{1,0:T(8,128)(2,1)} %get-tuple-element.8) | data formatting | bytes 2097152
  152.7 0.0 copy-done.1
  152.7 1.0 copy.18
  153.7 0.0 copy-done.2
  153.7 0.7 copy.19
  154.4 0.0 copy-done
  154.4 1.3 copy.20
Async XLA Ops:
  150.2 2.5 %copy-start.1 = (f32[256,1024]{1,0:T(8,128)S(1)}, f32[256,1024]{1,0:T(8,128)}, u32[]{:S(2)}) copy-start(f32[256,1024]{1,0:T(8,128)} %get-tuple-element.9) | copy-start | bytes 3145732
  150.3 3.4 %copy-start.2 = (f32[64,1024]{1,0:T(8,128)S(1)}, f32[64,1024]{1,0:T(8,128)}, u32[]{:S(2)}) copy-start(f32[64,1024]{1,0:T(8,128)} %get-tuple-element.10) | copy-start | bytes 786436
  150.3 4.1 %copy-start = (bf16[256,4096]{1,0:T(8,128)(2,1)S(1)}, bf16[256,4096]{1,0:T(8,128)(2,1)}, u32[]{:S(2)}) copy-start(bf16[256,4096]{1,0:T(8,128)(2,1)} %get-tuple-element.11) | copy-start | bytes 6291460

commit v4 on v3

v4 whole, which is shorter than its diff:
```python
import jax
import jax.numpy as jnp
from jax import lax
from jax.experimental import pallas as pl
from jax.experimental.pallas import tpu as pltpu
from jax.sharding import PartitionSpec as P

BF = jnp.bfloat16
F32 = jnp.float32
I32 = jnp.int32


def dot_nn(a, b):
    return lax.dot_general(a, b, (((1,), (0,)), ((), ())), preferred_element_type=F32)


def dot_nt(a, b):
    return lax.dot_general(a, b, (((1,), (1,)), ((), ())), preferred_element_type=F32)


def dot_tn(a, b):
    return lax.dot_general(a, b, (((0,), (0,)), ((), ())), preferred_element_type=F32)


def three(x):
    a = x.astype(BF)
    rest = x - a.astype(F32)
    b = rest.astype(BF)
    c = (rest - b.astype(F32)).astype(BF)
    return a, b, c


def iota(shape, dim):
    return lax.broadcasted_iota(I32, shape, dim)

MESH = pl.DeviceIdType.MESH
NEAR = (1, 3, 2)


class Copies:
    def __init__(self, send_sems, recv_sems):
        self.send_sems, self.recv_sems = send_sems, recv_sems
        self.copies, self.got = [], []
        self.used = 0

    def take(self, number):
        self.used += number
        assert self.used <= self.send_sems.shape[0]
        return self.used - number

    def send(self, src, dst, device):
        at = self.take(1)
        copy = pltpu.make_async_remote_copy(
            src_ref=src,
            dst_ref=dst,
            send_sem=self.send_sems.at[at],
            recv_sem=self.recv_sems.at[at],
            device_id=device,
            device_id_type=MESH,
        )
        copy.start()
        self.copies.append(copy)
        self.got.append(False)
        return len(self.copies) - 1

    def wait(self, *which):
        for i in which:
            if not self.got[i]:
                self.copies[i].wait_recv()
                self.got[i] = True

    def finish(self):
        self.wait(*range(len(self.copies)))
        for copy in self.copies:
            copy.wait_send()


def whole_kernel(
    own, rows_t, picks_t, grad, inputs, weight, keys, values,
    in_grad, w_grad, k_grad, t_grad,
    pay, mid, arr, inp, wt, key, val, acc, low, soft, score, wsend, wrecv, back, ret, spread,
    tpart, tcore, thalf, tz, placed, hsend, hrecv, lrecv, qg, gq, ginp, near, ksend, krecv, kfin,
    psend, precv, wfin, load_sem, ssem, rsem,
):
    heads, tokens = own.shape
    width = grad.shape[1]
    side, rows = pay.shape[1], pay.shape[3]
    shards = side * side
    lanes = picks_t.shape[0]
    blocks = 2 * heads
    top = lanes // blocks
    cols = acc.shape[1]
    half = cols // blocks
    count = key.shape[0]
    tiles = count // 128
    table_rows = val.shape[0]
    slots = 2 * shards * rows
    me, r = lax.axis_index("tab"), lax.axis_index("rep")
    mx, my = me // side, lax.rem(me, side)
    mz, mc = r // 2, lax.rem(r, 2)
    mate = {"rep": mz * 2 + 1 - mc}
    copies = Copies(ssem, rsem)
    send, wait = copies.send, copies.wait

    def up(at, by):
        return lax.rem(at + by + side, side)

    def tab(dx, dy):
        return up(mx, dx) * side + up(my, dy)

    def at_z(d):
        return {"rep": up(mz, d) * 2 + mc}

    loads = [pltpu.make_async_copy(inputs, inp, load_sem.at[0])]
    depth = width // 4
    for i in range(4):
        piece = pl.ds(i * depth, depth)
        loads.append(pltpu.make_async_copy(weight.at[piece], wt.at[piece], load_sem.at[1 + i]))
    loads.append(pltpu.make_async_copy(keys, key, load_sem.at[5]))
    loads.append(pltpu.make_async_copy(values, val, load_sem.at[6]))
    for load in loads:
        load.start()
    barrier = pltpu.get_barrier_semaphore()
    for d in range(1, shards):
        pl.semaphore_signal(
            barrier, inc=1, device_id={"tab": lax.rem(me + d, shards)}, device_id_type=MESH
        )
    for d in range(1, 8):
        pl.semaphore_signal(
            barrier, inc=1, device_id={"rep": lax.rem(r + d, 8)}, device_id_type=MESH
        )

    owned = jnp.concatenate([own[h : h + 1, :] for h in range(heads)], axis=1)
    messages = heads * tokens
    across = jnp.broadcast_to(owned, (messages, messages))
    same = across == across.T
    earlier = iota((messages, messages), 0) < iota((messages, messages), 1)
    rank = jnp.sum(jnp.where(same & earlier, 1.0, 0.0), axis=0, keepdims=True).astype(I32)
    place = (rank // rows) * (shards * rows) + owned * rows + rank % rows

    def hit_rows(part):
        at = iota((shards * rows, messages), 0) + part * shards * rows
        return jnp.where(at == place, 1.0, 0.0)

    phase_one = {}
    for part in range(2):
        hit = hit_rows(part)
        either = hit[:, :tokens]
        for h in range(1, heads):
            either = either + hit[:, h * tokens : (h + 1) * tokens]
        either = either.astype(BF)
        for at in range(0, width, 512):
            block = dot_nn(either, grad[:, at : at + 512]).astype(BF)
            pay[part, :, :, :, at : at + 512] = block.reshape(side, side, rows, 512)
        if part == 0:
            pl.semaphore_wait(barrier, shards + 6)
        for d in NEAR:
            for e in (0,) + NEAR:
                if part == 0:
                    src, device = pay.at[0, up(mx, e), up(my, d)], {"tab": tab(0, d)}
                    onward = mid.at[0, my, up(mx, e)]
                else:
                    src, device = pay.at[1, up(mx, d), up(my, e)], {"tab": tab(d, 0)}
                    onward = mid.at[1, mx, up(my, e)]
                dst = onward if e else arr.at[part, me]
                phase_one[part, d, e] = send(src, dst, device)
    phase_two = {}

    def pass_on(part, d, e):
        if part == 0:
            src = mid.at[0, up(my, -d), up(mx, e)] if d else pay.at[0, up(mx, e), my]
            dst, device = arr.at[0, tab(0, -d)], {"tab": tab(e, 0)}
        else:
            src = mid.at[1, up(mx, -d), up(my, e)] if d else pay.at[1, mx, up(my, e)]
            dst, device = arr.at[1, tab(-d, 0)], {"tab": tab(0, e)}
        phase_two[part, d, e] = send(src, dst, device)

    for part in range(2):
        for e in NEAR:
            pass_on(part, 0, e)
        arr[part, me] = pay[part, mx, my]

    loads[0].wait()
    for i in range(4):
        loads[1 + i].wait()
        piece = dot_nn(inp[:, i * depth : (i + 1) * depth], wt[i * depth : (i + 1) * depth, :])
        acc[...] = piece if i == 0 else acc[...] + piece
    low[...] = acc[...].astype(BF)
    lows = []
    for d in range(1, 8):
        p = lax.rem(r + d, 8)
        piece = pl.ds(pl.multiple_of((p // 2) * half, half), half)
        lows.append(send(low.at[:, piece], lrecv.at[r], {"rep": p}))
    lrecv[r] = low[:, pl.ds(pl.multiple_of(mz * half, half), half)]
    pick = picks_t[...].T
    low_pick = pick % 128
    high_pick = pick // 128
    lane_block = iota((tokens, lanes), 1) // top
    head_of = lane_block // 2
    chosen = jnp.zeros((tokens, lanes), F32)
    loads[5].wait()
    for b in range(blocks):
        parts = three(acc[:, b * half : (b + 1) * half])
        for j in range(tiles):
            names = key[j * 128 : (j + 1) * 128, b * half : (b + 1) * half]
            part = dot_nt(parts[2], names) + dot_nt(parts[1], names) + dot_nt(parts[0], names)
            got = jnp.take_along_axis(part, low_pick, axis=1)
            chosen = jnp.where((high_pick == j) & (lane_block == b), got, chosen)
    even = lane_block % 2 == 0
    other = jnp.where(
        even, pltpu.roll(chosen, lanes - top, axis=1), pltpu.roll(chosen, top, axis=1)
    )
    scores = chosen + other

    def over_heads(x, fill, reduce):
        out = jnp.zeros((tokens, lanes), F32)
        for h in range(heads):
            one = reduce(jnp.where(head_of == h, x, fill), axis=1, keepdims=True)
            out = jnp.where(head_of == h, one, out)
        return out

    raised = jnp.exp(scores - over_heads(scores, -jnp.inf, jnp.max))
    weights = raised / (over_heads(raised, 0.0, jnp.sum) * 0.5)
    soft[...] = weights
    low_soft = weights.astype(BF).astype(F32)

    def hits(h):
        column = jnp.broadcast_to(place[:, h * tokens : (h + 1) * tokens], (tokens, tokens)).T
        column = jnp.concatenate([column] * (slots // tokens), axis=1)
        return jnp.where(iota((tokens, slots), 1) == column, 1.0, 0.0).astype(BF)

    sent = jnp.zeros((slots, 2 * lanes), F32)
    for h in range(heads):
        one = rows_t[h * top : (h + 1) * top, :].astype(F32)
        numbers = jnp.concatenate([one] * blocks, axis=0).T
        turned = low_soft if h == 0 else pltpu.roll(low_soft, lanes - h * 2 * top, axis=1)
        sent = sent + dot_tn(hits(h), jnp.concatenate([numbers, turned], axis=1).astype(BF))
    wsend[...] = sent.astype(BF).reshape(2, shards, rows, 2 * lanes)

    def pass_all(d):
        for e in (0,) + NEAR:
            for part in range(2):
                wait(phase_one[part, d, e])
                if e:
                    pass_on(part, d, e)

    pass_all(1)
    weighing = []
    for dx in range(side):
        for dy in range(side):
            if dx or dy:
                p = tab(dx, dy)
                weighing.append(send(wsend.at[:, p], wrecv.at[:, me], {"tab": p}))
    wrecv[:, me] = wsend[:, me]
    pass_all(3)
    pass_all(2)

    wait(*weighing)
    band = 128
    per_band = band // rows

    def spread_band(g, carry):
        part, at = g // (shards // per_band), lax.rem(g, shards // per_band) * per_band
        block = wrecv[part, pl.ds(at, per_band)].reshape(band, 2 * lanes).astype(F32)
        row_t, soft_t = block[:, :lanes].T, block[:, lanes:].T
        names = iota((table_rows, band), 0).astype(F32)
        held = jnp.zeros((table_rows, band), F32)
        for k in range(top):
            held = held + jnp.where(names == row_t[k : k + 1], soft_t[k : k + 1], 0.0)
        spread[:, pl.ds(pl.multiple_of(g * band, band), band)] = held.astype(BF)
        return carry

    lax.fori_loop(0, slots // band, spread_band, 0)

    loads[6].wait()
    for d in (0,) + NEAR:
        for e in NEAR:
            for part in range(2):
                wait(phase_two[part, d, e])
    for part in range(2):
        for q in range(0, shards, per_band):
            here = slice(q, q + per_band)
            product = dot_nt(arr[part, here].reshape(band, width), val[...])
            name = wrecv[part, here, :, :lanes].reshape(band, lanes).astype(I32)
            out = jnp.zeros((band, lanes), F32)
            for j in range(table_rows // 128):
                got = jnp.take_along_axis(product[:, j * 128 : (j + 1) * 128], name % 128, axis=1)
                out = jnp.where(name // 128 == j, got, out)
            back[part, here] = out.reshape(per_band, rows, lanes)
    returning = []
    for dx in range(side):
        for dy in range(side):
            if dx or dy:
                p = tab(dx, dy)
                returning.append(send(back.at[:, p], ret.at[:, me], {"tab": p}))
    ret[:, me] = back[:, me]
    spreading = []
    piece_width = width // shards
    for dx in (0,) + NEAR:
        for dy in (0,) + NEAR:
            if dx or dy:
                p = tab(dx, dy)
                piece = pl.ds(pl.multiple_of(p * piece_width, piece_width), piece_width)
                spreading.append(send(inp.at[:, piece], ginp.at[me], {"tab": p}))
    ginp[me] = inp[:, pl.ds(pl.multiple_of(me * piece_width, piece_width), piece_width)]

    own_half = table_rows // 2
    quarter = own_half // 4
    for at in range(0, width, 512):
        column = arr[:, :, :, at : at + 512].reshape(slots, 512)
        tpart[:, at : at + 512] = dot_nn(spread[...], column).astype(BF)
    swaps = {}
    for d in NEAR + (0,):
        z = up(mz, d)
        row = pl.multiple_of((1 - mc) * own_half + z * quarter, quarter)
        swaps[d] = send(tpart.at[pl.ds(row, quarter)], tcore.at[z], mate)

    wait(*returning)
    parts = three(ret[...].reshape(slots, lanes))
    slot_grad = jnp.zeros((tokens, lanes), F32)
    for h in range(heads):
        hit = hits(h)
        got = dot_nn(hit, parts[2]) + dot_nn(hit, parts[1]) + dot_nn(hit, parts[0])
        slot_grad = jnp.where(head_of == h, got, slot_grad)
    weights = soft[...]
    mean = over_heads(weights * slot_grad, 0.0, jnp.sum) * 0.5
    score[0] = weights * (slot_grad - mean)
    score[1] = low_pick.astype(F32)
    score[2] = (high_pick + tiles * lane_block).astype(F32)

    def place_band(i, carry):
        here = pl.ds(pl.multiple_of(i * 8, 8), 8)
        amount, low8, high8 = score[0, here, :], score[1, here, :], score[2, here, :]
        high_names = iota((blocks * tiles, lanes), 0).astype(F32)
        low_names = iota((128, lanes), 0).astype(F32)
        for u in range(8):
            left = jnp.where(high_names == high8[u : u + 1], amount[u : u + 1], 0.0).astype(BF)
            right = jnp.where(low_names == low8[u : u + 1], 1.0, 0.0).astype(BF)
            placed[i * 8 + u] = dot_nt(left, right)
        return carry

    lax.fori_loop(0, tokens // 8, place_band, 0)
    first, second = {}, {}

    def crossed(b, one, two):
        return tab(two, one) if b % 2 == 0 else tab(one, two)

    def part_on(b, e, d):
        at = crossed(b, -e, 0)
        src = gq.at[b, at] if e else qg.at[b]
        second[b, e, d] = send(src, gq.at[b, at], {"tab": crossed(b, 0, d)})

    for b in range(blocks):
        total = jnp.zeros((tokens, half), F32)
        for j in range(tiles):
            sums = placed[:, b * tiles + j, :].astype(BF)
            hsend[2 * b + j % 2, :, (j // 2) * 128 : (j // 2 + 1) * 128] = sums
            total = total + dot_nn(sums, key[j * 128 : (j + 1) * 128, b * half : (b + 1) * half])
        qg[b] = total.astype(BF)
        gq[b, me] = total.astype(BF)
        for d in (1, -1, 2):
            first[b, d] = send(qg.at[b], gq.at[b, me], {"tab": crossed(b, d, 0)})
        if b < 2:
            for d in (1, -1):
                part_on(b, 0, d)

    table_in = {}
    for d in NEAR + (0,):
        z = up(mz, d)
        wait(swaps[d])
        row = pl.multiple_of(mc * own_half + z * quarter, quarter)
        thalf[z] = (tpart[pl.ds(row, quarter), :].astype(F32) + tcore[z].astype(F32)).astype(BF)
        if d:
            table_in[d] = send(thalf.at[z], tz.at[mz], at_z(d))
        else:
            tz[mz] = thalf[mz]
    halves = []
    for d in range(1, 8):
        p = lax.rem(r + d, 8)
        halves.append(send(hsend.at[p], hrecv.at[r], {"rep": p}))
    hrecv[r] = hsend[r]

    def cross(pair):
        for e in (1, -1, 2):
            for b in pair:
                wait(first[b, e])
                for d in (1, -1):
                    part_on(b, e, d)

    def round_again(pair):
        for e, d in ((0, 1), (1, 1), (-1, -1), (2, -1)):
            for b in pair:
                wait(second[b, e, d])
                at = crossed(b, -e, -d)
                block = gq.at[b, at]
                second[b, e, 2 * d] = send(block, block, {"tab": crossed(b, 0, d)})

    def whole_pair(pair):
        for (b, e, d), copy in list(second.items()):
            if b in pair:
                wait(copy)

    cross((0, 1))
    for b in (2, 3):
        for d in (1, -1):
            part_on(b, 0, d)
    joined = jnp.concatenate([qg[b] for b in range(blocks)], axis=1)
    for at in range(0, width, 512):
        in_grad[:, at : at + 512] = dot_nt(joined, wt[at : at + 512, :]).astype(BF)
    round_again((0, 1))
    cross((2, 3))
    wait(*spreading)

    def turn(q, carry):
        near[:, pl.ds(pl.multiple_of(q * tokens, tokens), tokens)] = ginp[q].astype(F32).T.astype(BF)
        return carry

    lax.fori_loop(0, shards, turn, 0)

    share = piece_width // 8
    sums_in = {}

    def weigh(pair, n):
        whole_pair(pair)
        for i, b in enumerate(pair):
            part = dot_nn(near[...], gq[b].reshape(shards * tokens, half)).astype(BF)
            psend[n, :, :, i * half : (i + 1) * half] = part.reshape(8, share, half)
        sums_in[n] = []
        for d in range(1, 8):
            p = lax.rem(r + d, 8)
            sums_in[n].append(send(psend.at[n, p], precv.at[n, r], {"rep": p}))
        precv[n, r] = psend[n, r]

    weigh((0, 1), 0)
    round_again((2, 3))
    wait(*table_in.values())
    summed = tz[0].astype(F32)
    for z in range(1, 4):
        summed = summed + tz[z].astype(F32)

    def table_rows_of(z):
        return t_grad.at[pl.ds(pl.multiple_of(mc * own_half + z * quarter, quarter), quarter)]

    table_mine = table_rows_of(mz)
    table_mine[...] = summed.astype(BF)
    table_out = {d: send(table_mine, table_mine, at_z(d)) for d in (1, -1)}
    send(table_mine, table_mine, mate)

    wait(*lows, *halves)
    key_part = dot_tn(
        hrecv[...].reshape(8 * tokens, count // 2), lrecv[...].reshape(8 * tokens, half)
    )
    key_rows = count // shards
    ksend[...] = key_part.astype(BF).reshape(8, key_rows, half)
    key_base = copies.take(shards)
    key_out = []
    for i in range(2):
        for dx in range(side):
            x = lax.rem(mx + dx, side)
            copy = pltpu.make_async_remote_copy(
                src_ref=ksend.at[x * 2 + i],
                dst_ref=krecv.at[me],
                send_sem=ssem.at[key_base + i * side + dx],
                recv_sem=rsem.at[key_base + me],
                device_id={"tab": x * side + 2 * mc + i},
                device_id_type=MESH,
            )
            key_out.append((i, dx, copy))
            if dx:
                copy.start()
            else:

                @pl.when(my != 2 * mc + i)
                def _(copy=copy):
                    copy.start()

                @pl.when(my == 2 * mc + i)
                def _(x=x, i=i):
                    krecv[me] = ksend[x * 2 + i]

    before, after = table_rows_of(up(mz, -1)), table_rows_of(up(mz, 1))
    wait(table_out[1])
    lower = before.at[pl.ds(0, quarter // 2)]
    send(lower, lower, at_z(1))
    send(before, before, mate)
    wait(table_out[-1])
    upper = after.at[pl.ds(quarter // 2, quarter // 2)]
    send(upper, upper, at_z(-1))
    send(after, after, mate)
    table_far = [len(copies.copies) - 4, len(copies.copies) - 2]

    weigh((2, 3), 1)
    key_last = copies.take(8)
    keeper = my // 2

    def key_share(d):
        return pltpu.make_async_remote_copy(
            src_ref=kfin.at[mz],
            dst_ref=kfin.at[mz],
            send_sem=ssem.at[key_last + d],
            recv_sem=rsem.at[key_last + mz],
            device_id={"rep": lax.rem(r + d, 8)},
            device_id_type=MESH,
        )

    @pl.when(keeper == mc)
    def _():
        for d in range(1, shards):
            q = lax.rem(me + d, shards)
            pltpu.make_async_remote_copy(
                src_ref=ksend.at[0],
                dst_ref=krecv.at[q],
                send_sem=ssem.at[key_base],
                recv_sem=rsem.at[key_base + q],
                device_id={"tab": q},
                device_id_type=MESH,
            ).wait_recv()
        total = krecv[0].astype(F32)
        for q in range(1, shards):
            total = total + krecv[q].astype(F32)
        kfin[mz] = total.astype(BF)
        for d in range(1, 8):
            key_share(d).start()

    sums_out = {}
    for n in range(2):
        wait(*sums_in[n])
        total = precv[n, 0].astype(F32)
        for q in range(1, 8):
            total = total + precv[n, q].astype(F32)
        wfin[n, r] = total.astype(BF)
        mine = wfin.at[n, r]
        for d in NEAR:
            sums_out[n, d] = send(mine, mine, at_z(d))
        send(mine, mine, mate)
    wait(*table_far)
    across_z = table_rows_of(up(mz, 2))
    send(across_z, across_z, mate)
    for n in range(2):
        for d in NEAR:
            wait(sums_out[n, d])
            part = wfin.at[n, up(mz, -d) * 2 + mc]
            send(part, part, mate)

    for b in range(4):

        @pl.when((b != mz) | (keeper != mc))
        def _(b=b):
            pltpu.make_async_remote_copy(
                src_ref=kfin.at[b],
                dst_ref=kfin.at[b],
                send_sem=ssem.at[key_last],
                recv_sem=rsem.at[key_last + b],
                device_id=mate,
                device_id_type=MESH,
            ).wait_recv()

    for b in range(4):
        k_grad[:, b * half : (b + 1) * half] = kfin[b].astype(F32)
    wait(*range(len(copies.copies)))
    for n in range(2):
        done = wfin[n].reshape(piece_width, 2 * half).astype(F32)
        w_grad[:, n * 2 * half : (n + 1) * 2 * half] = done
    for i, dx, copy in key_out:
        if dx:
            copy.wait_send()
        else:

            @pl.when(my != 2 * mc + i)
            def _(copy=copy):
                copy.wait_send()

    @pl.when(keeper == mc)
    def _():
        for d in range(1, 8):
            key_share(d).wait_send()

    copies.finish()


def deliver_kernel(*refs):
    number = len(refs) // 2
    for i in range(number):
        refs[number + i][...] = refs[i][...]


def sds(shape, dtype):
    return jax.ShapeDtypeStruct(shape, dtype)


def on_device(inputs, grad_out, query_weight, sub_keys, values, owner, slot_rows, sub_index):
    tokens, width = inputs.shape
    cols = query_weight.shape[1]
    count = sub_keys.shape[0]
    heads, top = slot_rows.shape[1:]
    blocks = 2 * heads
    lanes = blocks * top
    half = cols // blocks
    shards = lax.axis_size("tab")
    side = 4
    rows = tokens * heads // shards
    slots = 2 * shards * rows
    table_rows = values.shape[0]
    own = jnp.transpose(owner, (1, 2, 0)).reshape(heads, tokens)
    rows_t = jnp.transpose(slot_rows, (1, 2, 0)).reshape(heads * top, tokens)
    picks_t = jnp.transpose(sub_index, (1, 2, 3, 0)).reshape(lanes, tokens)
    vmem = pl.BlockSpec(memory_space=pltpu.VMEM)
    anywhere = pl.BlockSpec(memory_space=pl.ANY)
    V = pltpu.VMEM
    shapes = (
        sds((tokens, width), BF),
        sds((width // shards, cols), F32),
        sds((count // shards, cols), F32),
        sds((table_rows, width), BF),
    )
    results = pl.pallas_call(
        whole_kernel,
        out_shape=shapes,
        in_specs=[vmem] * 4 + [anywhere] * 4,
        out_specs=(vmem,) * 4,
        scratch_shapes=[
            V((2, side, side, rows, width), BF),
            V((2, side, side, rows, width), BF),
            V((2, shards, rows, width), BF),
            V((tokens, width), BF),
            V((width, cols), BF),
            V((count, cols), BF),
            V((table_rows, width), BF),
            V((tokens, cols), F32),
            V((tokens, cols), BF),
            V((tokens, lanes), F32),
            V((3, tokens, lanes), F32),
            V((2, shards, rows, 2 * lanes), BF),
            V((2, shards, rows, 2 * lanes), BF),
            V((2, shards, rows, lanes), F32),
            V((2, shards, rows, lanes), F32),
            V((table_rows, slots), BF),
            V((table_rows, width), BF),
            V((4, table_rows // 8, width), BF),
            V((4, table_rows // 8, width), BF),
            V((4, table_rows // 8, width), BF),
            V((tokens, blocks * count // 128, 128), F32),
            V((8, tokens, count // 2), BF),
            V((8, tokens, count // 2), BF),
            V((8, tokens, half), BF),
            V((blocks, tokens, half), BF),
            V((blocks, shards, tokens, half), BF),
            V((shards, tokens, width // shards), BF),
            V((width // shards, shards * tokens), BF),
            V((8, count // shards, half), BF),
            V((shards, count // shards, half), BF),
            V((4, count // shards, half), BF),
            V((2, 8, width // shards // 8, 2 * half), BF),
            V((2, 8, width // shards // 8, 2 * half), BF),
            V((2, 8, width // shards // 8, 2 * half), BF),
            pltpu.SemaphoreType.DMA((7,)),
            pltpu.SemaphoreType.DMA((288,)),
            pltpu.SemaphoreType.DMA((288,)),
        ],
        compiler_params=pltpu.CompilerParams(
            collective_id=0, has_side_effects=True, vmem_limit_bytes=60 * 1024 * 1024
        ),
        name="whole",
    )(own, rows_t, picks_t, grad_out, inputs, query_weight, sub_keys, values)
    steps = 4
    specs = [pl.BlockSpec((x.shape[0] // steps, x.shape[1]), lambda i: (i, 0)) for x in shapes]
    return pl.pallas_call(
        deliver_kernel,
        out_shape=shapes,
        grid=(steps,),
        in_specs=specs,
        out_specs=tuple(specs),
        name="deliver",
    )(*results)


def solution(mesh):
    placed = (
        P(("rep", "tab"), None),
        P(("rep", "tab"), None),
        P(),
        P(),
        P("tab", None),
        P(("rep", "tab"), None, None),
        P(("rep", "tab"), None, None),
        P(("rep", "tab"), None, None, None),
    )
    return jax.shard_map(
        on_device,
        mesh=mesh,
        in_specs=placed,
        out_specs=(P(("rep", "tab"), None), P("tab", None), P("tab", None), P("tab", None)),
        check_vma=False,
    )
```

time: 156 us -> 136 us (0.87)
  Pallas kernels: 150 us -> 135 us
  local copies, waits for them, and re-layouts: 5.44 us -> 0 us
    pallas_call x1 -> x2, Pallas kernels: 150 us -> 135 us  [the longest x1 130 us: on_device(): pl.pallas_call(whole_kernel, out_shape=shapes, in_specs=[vmem] * 4 + [any...]
    unnamed x10 -> x0, local copies, waits for them, and re-layouts: 5.44 us -> none
where the time goes in v4:
time: 136 us
  Pallas kernels  135 us (99%)
    pallas_call x1, Pallas kernels, on_device(): pl.pallas_call(whole_kernel, out_shape=shapes, in_specs=[vmem] * 4 + [any...  130 us
    pallas_call x1, Pallas kernels, on_device(): pl.pallas_call(deliver_kernel, out_shape=shapes, grid=(steps,), in_specs=...  4.83 us

profile of v4, /device:TPU:1, one launch (start us, length us, event | category | flops | bytes accessed | tf_op | source)
XLA Modules:
  0.0 135.8 jit_solution(15285081704715289064)
XLA Ops:
  0.6 130.3 %whole.1 = (bf16[128,4096]{1,0:T(8,128)(2,1)}, f32[256,1024]{1,0:T(8,128)}, f32[64,1024]{1,0:T(8,128)}, bf16[256,4096]{1,0:T(8,128)(2,1)}) custom-call(s32[2,128]{1,0:T(2,128)} %bitcast.13, s32[64,128]{1,0:T(8,128)} %bitcast.12, s32[128,128]{1,0:T(8,128)} %bitcast.11, bf16[128,4096]{1,0:T(8,128)(2,1)} %grad.1, bf16[128,4096]{1,0:T(8,128)(2,1)} %inputs.1, ...), custom_call_target="tpu_custom_call" | custom-call | tf_op jit(solution)/shard_map/whole/pallas_call | solution.py:616
  130.9 4.8 %deliver.1 = (bf16[128,4096]{1,0:T(8,128)(2,1)}, f32[256,1024]{1,0:T(8,128)}, f32[64,1024]{1,0:T(8,128)}, bf16[256,4096]{1,0:T(8,128)(2,1)}) custom-call(bf16[128,4096]{1,0:T(8,128)(2,1)} %get-tuple-element.8.refs_0_, f32[256,1024]{1,0:T(8,128)} %get-tuple-element.9.refs_1_, f32[64,1024]{1,0:T(8,128)} %get-tuple-element.10.refs_2_, ...), custom_call_target="tpu_custom_call" | custom-call | tf_op jit(solution)/shard_map/deliver/pallas_call | solution.py:667

commit v5 on v4

--- a/solution.py
+++ b/solution.py
@@ -324,22 +324,35 @@
         slot_grad = jnp.where(head_of == h, got, slot_grad)
     weights = soft[...]
     mean = over_heads(weights * slot_grad, 0.0, jnp.sum) * 0.5
-    score[0] = weights * (slot_grad - mean)
-    score[1] = low_pick.astype(F32)
-    score[2] = (high_pick + tiles * lane_block).astype(F32)
-
-    def place_band(i, carry):
-        here = pl.ds(pl.multiple_of(i * 8, 8), 8)
-        amount, low8, high8 = score[0, here, :], score[1, here, :], score[2, here, :]
-        high_names = iota((blocks * tiles, lanes), 0).astype(F32)
-        low_names = iota((128, lanes), 0).astype(F32)
-        for u in range(8):
-            left = jnp.where(high_names == high8[u : u + 1], amount[u : u + 1], 0.0).astype(BF)
-            right = jnp.where(low_names == low8[u : u + 1], 1.0, 0.0).astype(BF)
-            placed[i * 8 + u] = dot_nt(left, right)
-        return carry
-
-    lax.fori_loop(0, tokens // 8, place_band, 0)
+    score_grad = weights * (slot_grad - mean)
+    pairs = tokens // 2
+    early_lanes = iota((pairs, lanes), 1) < lanes // 2
+
+    def place_head(h):
+        def pack(x):
+            turned = pltpu.roll(x, lanes // 2, axis=1)
+            one, two = (x, turned) if h == 0 else (turned, x)
+            return jnp.where(early_lanes, one[:pairs], two[pairs:])
+
+        score[0] = pack(score_grad)
+        score[1] = pack(low_pick.astype(F32))
+        score[2] = pack(high_pick.astype(F32)) + (tiles * lane_block[:pairs]).astype(F32)
+
+        def place_band(i, carry):
+            here = pl.ds(pl.multiple_of(i * 8, 8), 8)
+            amount, low8, high8 = score[0, here, :], score[1, here, :], score[2, here, :]
+            high_names = iota((blocks * tiles, lanes), 0).astype(F32)
+            low_names = iota((128, lanes), 0).astype(F32)
+            for u in range(8):
+                left = jnp.where(high_names == high8[u : u + 1], amount[u : u + 1], 0.0).astype(BF)
+                right = jnp.where(low_names == low8[u : u + 1], 1.0, 0.0).astype(BF)
+                sums = dot_nt(left, right)
+                placed[i * 8 + u] = sums[: 2 * tiles]
+                placed[i * 8 + u + pairs] = sums[2 * tiles :]
+            return carry
+
+        lax.fori_loop(0, pairs // 8, place_band, 0)
+
     first, second = {}, {}
 
     def crossed(b, one, two):
@@ -350,10 +363,13 @@
         src = gq.at[b, at] if e else qg.at[b]
         second[b, e, d] = send(src, gq.at[b, at], {"tab": crossed(b, 0, d)})
 
+    table_in = {}
     for b in range(blocks):
+        if b % 2 == 0:
+            place_head(b // 2)
         total = jnp.zeros((tokens, half), F32)
         for j in range(tiles):
-            sums = placed[:, b * tiles + j, :].astype(BF)
+            sums = placed[:, b % 2 * tiles + j, :].astype(BF)
             hsend[2 * b + j % 2, :, (j // 2) * 128 : (j // 2 + 1) * 128] = sums
             total = total + dot_nn(sums, key[j * 128 : (j + 1) * 128, b * half : (b + 1) * half])
         qg[b] = total.astype(BF)
@@ -363,17 +379,19 @@
         if b < 2:
             for d in (1, -1):
                 part_on(b, 0, d)
-
-    table_in = {}
-    for d in NEAR + (0,):
-        z = up(mz, d)
-        wait(swaps[d])
-        row = pl.multiple_of(mc * own_half + z * quarter, quarter)
-        thalf[z] = (tpart[pl.ds(row, quarter), :].astype(F32) + tcore[z].astype(F32)).astype(BF)
-        if d:
-            table_in[d] = send(thalf.at[z], tz.at[mz], at_z(d))
-        else:
-            tz[mz] = thalf[mz]
+        if b != 1:
+            continue
+        for d in NEAR + (0,):
+            z = up(mz, d)
+            wait(swaps[d])
+            row = pl.multiple_of(mc * own_half + z * quarter, quarter)
+            joint = tpart[pl.ds(row, quarter), :].astype(F32) + tcore[z].astype(F32)
+            thalf[z] = joint.astype(BF)
+            if d:
+                table_in[d] = send(thalf.at[z], tz.at[mz], at_z(d))
+            else:
+                tz[mz] = thalf[mz]
+
     halves = []
     for d in range(1, 8):
         p = lax.rem(r + d, 8)
@@ -409,6 +427,18 @@
         in_grad[:, at : at + 512] = dot_nt(joined, wt[at : at + 512, :]).astype(BF)
     round_again((0, 1))
     cross((2, 3))
+    wait(*table_in.values())
+    summed = tz[0].astype(F32)
+    for z in range(1, 4):
+        summed = summed + tz[z].astype(F32)
+
+    def table_rows_of(z):
+        return t_grad.at[pl.ds(pl.multiple_of(mc * own_half + z * quarter, quarter), quarter)]
+
+    table_mine = table_rows_of(mz)
+    table_mine[...] = summed.astype(BF)
+    table_out = {d: send(table_mine, table_mine, at_z(d)) for d in (1, -1)}
+    send(table_mine, table_mine, mate)
     wait(*spreading)
 
     def turn(q, carry):
@@ -433,18 +463,6 @@
 
     weigh((0, 1), 0)
     round_again((2, 3))
-    wait(*table_in.values())
-    summed = tz[0].astype(F32)
-    for z in range(1, 4):
-        summed = summed + tz[z].astype(F32)
-
-    def table_rows_of(z):
-        return t_grad.at[pl.ds(pl.multiple_of(mc * own_half + z * quarter, quarter), quarter)]
-
-    table_mine = table_rows_of(mz)
-    table_mine[...] = summed.astype(BF)
-    table_out = {d: send(table_mine, table_mine, at_z(d)) for d in (1, -1)}
-    send(table_mine, table_mine, mate)
 
     wait(*lows, *halves)
     key_part = dot_tn(
@@ -522,7 +540,6 @@
         for d in range(1, 8):
             key_share(d).start()
 
-    sums_out = {}
     for n in range(2):
         wait(*sums_in[n])
         total = precv[n, 0].astype(F32)
@@ -530,17 +547,11 @@
             total = total + precv[n, q].astype(F32)
         wfin[n, r] = total.astype(BF)
         mine = wfin.at[n, r]
-        for d in NEAR:
-            sums_out[n, d] = send(mine, mine, at_z(d))
-        send(mine, mine, mate)
+        for d in range(1, 8):
+            send(mine, mine, {"rep": lax.rem(r + d, 8)})
     wait(*table_far)
     across_z = table_rows_of(up(mz, 2))
     send(across_z, across_z, mate)
-    for n in range(2):
-        for d in NEAR:
-            wait(sums_out[n, d])
-            part = wfin.at[n, up(mz, -d) * 2 + mc]
-            send(part, part, mate)
 
     for b in range(4):
 
@@ -629,7 +640,7 @@
             V((tokens, cols), F32),
             V((tokens, cols), BF),
             V((tokens, lanes), F32),
-            V((3, tokens, lanes), F32),
+            V((3, tokens // 2, lanes), F32),
             V((2, shards, rows, 2 * lanes), BF),
             V((2, shards, rows, 2 * lanes), BF),
             V((2, shards, rows, lanes), F32),
@@ -639,7 +650,7 @@
             V((4, table_rows // 8, width), BF),
             V((4, table_rows // 8, width), BF),
             V((4, table_rows // 8, width), BF),
-            V((tokens, blocks * count // 128, 128), F32),
+            V((tokens, 2 * count // 128, 128), F32),
             V((8, tokens, count // 2), BF),
             V((8, tokens, count // 2), BF),
             V((8, tokens, half), BF),

time: 136 us -> 131 us (0.963)
  Pallas kernels: 135 us -> 130 us
    pallas_call x1, Pallas kernels: 130 us -> 126 us  [on_device(): pl.pallas_call(whole_kernel, out_shape=shapes, in_specs=[vmem] * 4 + [any...]
where the time goes in v5:
time: 131 us
  Pallas kernels  130 us (99%)
    pallas_call x1, Pallas kernels, on_device(): pl.pallas_call(whole_kernel, out_shape=shapes, in_specs=[vmem] * 4 + [any...  126 us
    pallas_call x1, Pallas kernels, on_device(): pl.pallas_call(deliver_kernel, out_shape=shapes, grid=(steps,), in_specs=...  4.83 us

profile of v5, /device:TPU:1, one launch (start us, length us, event | category | flops | bytes accessed | tf_op | source)
XLA Modules:
  0.0 131.0 jit_solution(4999517789794752875)
XLA Ops:
  0.6 125.5 %whole.1 = (bf16[128,4096]{1,0:T(8,128)(2,1)}, f32[256,1024]{1,0:T(8,128)}, f32[64,1024]{1,0:T(8,128)}, bf16[256,4096]{1,0:T(8,128)(2,1)}) custom-call(s32[2,128]{1,0:T(2,128)} %bitcast.13, s32[64,128]{1,0:T(8,128)} %bitcast.12, s32[128,128]{1,0:T(8,128)} %bitcast.11, bf16[128,4096]{1,0:T(8,128)(2,1)} %grad.1, bf16[128,4096]{1,0:T(8,128)(2,1)} %inputs.1, ...), custom_call_target="tpu_custom_call" | custom-call | tf_op jit(solution)/shard_map/whole/pallas_call | solution.py:627
  126.2 4.8 %deliver.1 = (bf16[128,4096]{1,0:T(8,128)(2,1)}, f32[256,1024]{1,0:T(8,128)}, f32[64,1024]{1,0:T(8,128)}, bf16[256,4096]{1,0:T(8,128)(2,1)}) custom-call(bf16[128,4096]{1,0:T(8,128)(2,1)} %get-tuple-element.8.refs_0_, f32[256,1024]{1,0:T(8,128)} %get-tuple-element.9.refs_1_, f32[64,1024]{1,0:T(8,128)} %get-tuple-element.10.refs_2_, ...), custom_call_target="tpu_custom_call" | custom-call | tf_op jit(solution)/shard_map/deliver/pallas_call | solution.py:678

commit v6 on v5

--- a/solution.py
+++ b/solution.py
@@ -464,6 +464,8 @@
     weigh((0, 1), 0)
     round_again((2, 3))
 
+    weigh((2, 3), 1)
+
     wait(*lows, *halves)
     key_part = dot_tn(
         hrecv[...].reshape(8 * tokens, count // 2), lrecv[...].reshape(8 * tokens, half)
@@ -507,7 +509,6 @@
     send(after, after, mate)
     table_far = [len(copies.copies) - 4, len(copies.copies) - 2]
 
-    weigh((2, 3), 1)
     key_last = copies.take(8)
     keeper = my // 2
 

time: 131 us -> 131 us (level)
  no operation moved by 1% of the time
where the time goes in v6:
time: 131 us
  Pallas kernels  130 us (99%)
    pallas_call x1, Pallas kernels, on_device(): pl.pallas_call(whole_kernel, out_shape=shapes, in_specs=[vmem] * 4 + [any...  126 us
    pallas_call x1, Pallas kernels, on_device(): pl.pallas_call(deliver_kernel, out_shape=shapes, grid=(steps,), in_specs=...  4.83 us

profile of v6, /device:TPU:1, one launch (start us, length us, event | category | flops | bytes accessed | tf_op | source)
XLA Modules:
  0.0 131.0 jit_solution(16603517457089538624)
XLA Ops:
  0.6 125.5 %whole.1 = (bf16[128,4096]{1,0:T(8,128)(2,1)}, f32[256,1024]{1,0:T(8,128)}, f32[64,1024]{1,0:T(8,128)}, bf16[256,4096]{1,0:T(8,128)(2,1)}) custom-call(s32[2,128]{1,0:T(2,128)} %bitcast.13, s32[64,128]{1,0:T(8,128)} %bitcast.12, s32[128,128]{1,0:T(8,128)} %bitcast.11, bf16[128,4096]{1,0:T(8,128)(2,1)} %grad.1, bf16[128,4096]{1,0:T(8,128)(2,1)} %inputs.1, ...), custom_call_target="tpu_custom_call" | custom-call | tf_op jit(solution)/shard_map/whole/pallas_call | solution.py:628
  126.2 4.8 %deliver.1 = (bf16[128,4096]{1,0:T(8,128)(2,1)}, f32[256,1024]{1,0:T(8,128)}, f32[64,1024]{1,0:T(8,128)}, bf16[256,4096]{1,0:T(8,128)(2,1)}) custom-call(bf16[128,4096]{1,0:T(8,128)(2,1)} %get-tuple-element.8.refs_0_, f32[256,1024]{1,0:T(8,128)} %get-tuple-element.9.refs_1_, f32[64,1024]{1,0:T(8,128)} %get-tuple-element.10.refs_2_, ...), custom_call_target="tpu_custom_call" | custom-call | tf_op jit(solution)/shard_map/deliver/pallas_call | solution.py:679

commit v7 on v6

--- a/solution.py
+++ b/solution.py
@@ -1,3 +1,5 @@
+import functools
+
 import jax
 import jax.numpy as jnp
 from jax import lax
@@ -79,7 +81,7 @@
     own, rows_t, picks_t, grad, inputs, weight, keys, values,
     in_grad, w_grad, k_grad, t_grad,
     pay, mid, arr, inp, wt, key, val, acc, low, soft, score, wsend, wrecv, back, ret, spread,
-    tpart, tcore, thalf, tz, placed, hsend, hrecv, lrecv, qg, gq, ginp, near, ksend, krecv, kfin,
+    tpart, tcore, thalf, tz, tfold, placed, hsend, hrecv, lrecv, qg, gq, ginp, near, ksend, krecv, kfin,
     psend, precv, wfin, load_sem, ssem, rsem,
 ):
     heads, tokens = own.shape
@@ -310,7 +312,7 @@
         column = arr[:, :, :, at : at + 512].reshape(slots, 512)
         tpart[:, at : at + 512] = dot_nn(spread[...], column).astype(BF)
     swaps = {}
-    for d in NEAR + (0,):
+    for d in (2, 1, 3, 0):
         z = up(mz, d)
         row = pl.multiple_of((1 - mc) * own_half + z * quarter, quarter)
         swaps[d] = send(tpart.at[pl.ds(row, quarter)], tcore.at[z], mate)
@@ -363,6 +365,17 @@
         src = gq.at[b, at] if e else qg.at[b]
         second[b, e, d] = send(src, gq.at[b, at], {"tab": crossed(b, 0, d)})
 
+    def joint(d):
+        z = up(mz, d)
+        wait(swaps[d])
+        row = pl.multiple_of(mc * own_half + z * quarter, quarter)
+        return tpart[pl.ds(row, quarter), :].astype(F32) + tcore[z].astype(F32)
+
+    fold = quarter // 2
+    distant = up(mz, 2)
+    thalf[distant] = joint(2).astype(BF)
+    fold_up = send(thalf.at[distant, pl.ds(0, fold)], tfold.at[0], at_z(1))
+    fold_down = send(thalf.at[distant, pl.ds(fold, fold)], tfold.at[1], at_z(-1))
     table_in = {}
     for b in range(blocks):
         if b % 2 == 0:
@@ -381,16 +394,17 @@
                 part_on(b, 0, d)
         if b != 1:
             continue
-        for d in NEAR + (0,):
-            z = up(mz, d)
-            wait(swaps[d])
-            row = pl.multiple_of(mc * own_half + z * quarter, quarter)
-            joint = tpart[pl.ds(row, quarter), :].astype(F32) + tcore[z].astype(F32)
-            thalf[z] = joint.astype(BF)
-            if d:
-                table_in[d] = send(thalf.at[z], tz.at[mz], at_z(d))
-            else:
-                tz[mz] = thalf[mz]
+        whole = joint(1)
+        wait(fold_up)
+        thalf[up(mz, 1), :fold] = (whole[:fold] + tfold[0].astype(F32)).astype(BF)
+        thalf[up(mz, 1), fold:] = whole[fold:].astype(BF)
+        table_in[1] = send(thalf.at[up(mz, 1)], tz.at[0], at_z(1))
+        whole = joint(3)
+        wait(fold_down)
+        thalf[up(mz, -1), :fold] = whole[:fold].astype(BF)
+        thalf[up(mz, -1), fold:] = (whole[fold:] + tfold[1].astype(F32)).astype(BF)
+        table_in[3] = send(thalf.at[up(mz, -1)], tz.at[1], at_z(-1))
+        thalf[mz] = joint(0).astype(BF)
 
     halves = []
     for d in range(1, 8):
@@ -428,9 +442,7 @@
     round_again((0, 1))
     cross((2, 3))
     wait(*table_in.values())
-    summed = tz[0].astype(F32)
-    for z in range(1, 4):
-        summed = summed + tz[z].astype(F32)
+    summed = thalf[mz].astype(F32) + tz[0].astype(F32) + tz[1].astype(F32)
 
     def table_rows_of(z):
         return t_grad.at[pl.ds(pl.multiple_of(mc * own_half + z * quarter, quarter), quarter)]
@@ -548,8 +560,16 @@
             total = total + precv[n, q].astype(F32)
         wfin[n, r] = total.astype(BF)
         mine = wfin.at[n, r]
-        for d in range(1, 8):
-            send(mine, mine, {"rep": lax.rem(r + d, 8)})
+        if n == 0:
+            along = {d: send(mine, mine, at_z(d)) for d in NEAR}
+            send(mine, mine, mate)
+        else:
+            for d in range(1, 8):
+                send(mine, mine, {"rep": lax.rem(r + d, 8)})
+    for d in NEAR:
+        wait(along[d])
+        part = wfin.at[0, up(mz, -d) * 2 + mc]
+        send(part, part, mate)
     wait(*table_far)
     across_z = table_rows_of(up(mz, 2))
     send(across_z, across_z, mate)
@@ -590,10 +610,29 @@
     copies.finish()
 
 
-def deliver_kernel(*refs):
-    number = len(refs) // 2
-    for i in range(number):
-        refs[number + i][...] = refs[i][...]
+def deliver_kernel(pieces, *refs):
+    number = len(pieces)
+    sources, targets = refs[:number], refs[number : 2 * number]
+    held, sems = refs[2 * number : 3 * number], refs[-1]
+    moves = []
+    for i, count in enumerate(pieces):
+        size = held[i].shape[0] // count
+        for j in range(count):
+            here = pl.ds(j * size, size)
+            at = len(moves)
+            moves.append(
+                (
+                    pltpu.make_async_copy(sources[i].at[here], held[i].at[here], sems.at[0, at]),
+                    pltpu.make_async_copy(held[i].at[here], targets[i].at[here], sems.at[1, at]),
+                )
+            )
+    for fetch, _ in moves:
+        fetch.start()
+    for fetch, store in moves:
+        fetch.wait()
+        store.start()
+    for _, store in moves:
+        store.wait()
 
 
 def sds(shape, dtype):
@@ -650,7 +689,8 @@
             V((table_rows, width), BF),
             V((4, table_rows // 8, width), BF),
             V((4, table_rows // 8, width), BF),
-            V((4, table_rows // 8, width), BF),
+            V((2, table_rows // 8, width), BF),
+            V((2, table_rows // 16, width), BF),
             V((tokens, 2 * count // 128, 128), F32),
             V((8, tokens, count // 2), BF),
             V((8, tokens, count // 2), BF),
@@ -674,14 +714,14 @@
         ),
         name="whole",
     )(own, rows_t, picks_t, grad_out, inputs, query_weight, sub_keys, values)
-    steps = 4
-    specs = [pl.BlockSpec((x.shape[0] // steps, x.shape[1]), lambda i: (i, 0)) for x in shapes]
+    pieces = (4, 4, 1, 8)
     return pl.pallas_call(
-        deliver_kernel,
+        functools.partial(deliver_kernel, pieces),
         out_shape=shapes,
-        grid=(steps,),
-        in_specs=specs,
-        out_specs=tuple(specs),
+        in_specs=[anywhere] * 4,
+        out_specs=(anywhere,) * 4,
+        scratch_shapes=[V(x.shape, x.dtype) for x in shapes]
+        + [pltpu.SemaphoreType.DMA((2, sum(pieces)))],
         name="deliver",
     )(*results)
 

time: 131 us -> 130 us (level)
  no operation moved by 1% of the time
where the time goes in v7:
time: 130 us
  Pallas kernels  129 us (99%)
    pallas_call x1, Pallas kernels, on_device(): pl.pallas_call(whole_kernel, out_shape=shapes, in_specs=[vmem] * 4 + [any...  125 us
    pallas_call x1, Pallas kernels, on_device(): pl.pallas_call(functools.partial(deliver_kernel, pieces), out_shape=shape...  4.14 us

profile of v7, /device:TPU:1, one launch (start us, length us, event | category | flops | bytes accessed | tf_op | source)
XLA Modules:
  0.0 130.0 jit_solution(8121434533230641153)
XLA Ops:
  0.6 125.0 %whole.1 = (bf16[128,4096]{1,0:T(8,128)(2,1)}, f32[256,1024]{1,0:T(8,128)}, f32[64,1024]{1,0:T(8,128)}, bf16[256,4096]{1,0:T(8,128)(2,1)}) custom-call(s32[2,128]{1,0:T(2,128)} %bitcast.13, s32[64,128]{1,0:T(8,128)} %bitcast.12, s32[128,128]{1,0:T(8,128)} %bitcast.11, bf16[128,4096]{1,0:T(8,128)(2,1)} %grad.1, bf16[128,4096]{1,0:T(8,128)(2,1)} %inputs.1, ...), custom_call_target="tpu_custom_call" | custom-call | tf_op jit(solution)/shard_map/whole/pallas_call | solution.py:667
  125.7 4.1 %deliver.1 = (bf16[128,4096]{1,0:T(8,128)(2,1)}, f32[256,1024]{1,0:T(8,128)}, f32[64,1024]{1,0:T(8,128)}, bf16[256,4096]{1,0:T(8,128)(2,1)}) custom-call(bf16[128,4096]{1,0:T(8,128)(2,1)} %get-tuple-element.8.refs_0_, f32[256,1024]{1,0:T(8,128)} %get-tuple-element.9.refs_1_, f32[64,1024]{1,0:T(8,128)} %get-tuple-element.10.refs_2_, ...), custom_call_target="tpu_custom_call" | custom-call | tf_op jit(solution)/shard_map/deliver/pallas_call | solution.py:718

commit v8 on v7

--- a/solution.py
+++ b/solution.py
@@ -478,6 +478,17 @@
 
     weigh((2, 3), 1)
 
+    before, after = table_rows_of(up(mz, -1)), table_rows_of(up(mz, 1))
+    wait(table_out[1])
+    lower = before.at[pl.ds(0, quarter // 2)]
+    send(lower, lower, at_z(1))
+    send(before, before, mate)
+    wait(table_out[-1])
+    upper = after.at[pl.ds(quarter // 2, quarter // 2)]
+    send(upper, upper, at_z(-1))
+    send(after, after, mate)
+    table_far = [len(copies.copies) - 4, len(copies.copies) - 2]
+
     wait(*lows, *halves)
     key_part = dot_tn(
         hrecv[...].reshape(8 * tokens, count // 2), lrecv[...].reshape(8 * tokens, half)
@@ -509,17 +520,6 @@
                 @pl.when(my == 2 * mc + i)
                 def _(x=x, i=i):
                     krecv[me] = ksend[x * 2 + i]
-
-    before, after = table_rows_of(up(mz, -1)), table_rows_of(up(mz, 1))
-    wait(table_out[1])
-    lower = before.at[pl.ds(0, quarter // 2)]
-    send(lower, lower, at_z(1))
-    send(before, before, mate)
-    wait(table_out[-1])
-    upper = after.at[pl.ds(quarter // 2, quarter // 2)]
-    send(upper, upper, at_z(-1))
-    send(after, after, mate)
-    table_far = [len(copies.copies) - 4, len(copies.copies) - 2]
 
     key_last = copies.take(8)
     keeper = my // 2

time: 130 us -> 130 us (level)
  no operation moved by 1% of the time
where the time goes in v8:
time: 130 us
  Pallas kernels  129 us (99%)
    pallas_call x1, Pallas kernels, on_device(): pl.pallas_call(whole_kernel, out_shape=shapes, in_specs=[vmem] * 4 + [any...  125 us
    pallas_call x1, Pallas kernels, on_device(): pl.pallas_call(functools.partial(deliver_kernel, pieces), out_shape=shape...  4.14 us

profile of v8, /device:TPU:1, one launch (start us, length us, event | category | flops | bytes accessed | tf_op | source)
XLA Modules:
  0.0 130.0 jit_solution(12126041476641603034)
XLA Ops:
  0.6 125.1 %whole.1 = (bf16[128,4096]{1,0:T(8,128)(2,1)}, f32[256,1024]{1,0:T(8,128)}, f32[64,1024]{1,0:T(8,128)}, bf16[256,4096]{1,0:T(8,128)(2,1)}) custom-call(s32[2,128]{1,0:T(2,128)} %bitcast.13, s32[64,128]{1,0:T(8,128)} %bitcast.12, s32[128,128]{1,0:T(8,128)} %bitcast.11, bf16[128,4096]{1,0:T(8,128)(2,1)} %grad.1, bf16[128,4096]{1,0:T(8,128)(2,1)} %inputs.1, ...), custom_call_target="tpu_custom_call" | custom-call | tf_op jit(solution)/shard_map/whole/pallas_call | solution.py:667
  125.7 4.1 %deliver.1 = (bf16[128,4096]{1,0:T(8,128)(2,1)}, f32[256,1024]{1,0:T(8,128)}, f32[64,1024]{1,0:T(8,128)}, bf16[256,4096]{1,0:T(8,128)(2,1)}) custom-call(bf16[128,4096]{1,0:T(8,128)(2,1)} %get-tuple-element.8.refs_0_, f32[256,1024]{1,0:T(8,128)} %get-tuple-element.9.refs_1_, f32[64,1024]{1,0:T(8,128)} %get-tuple-element.10.refs_2_, ...), custom_call_target="tpu_custom_call" | custom-call | tf_op jit(solution)/shard_map/deliver/pallas_call | solution.py:718
